TPU v7x, 128 devices: a whole 4x4x4 slice. The times are simulated.
128 devices in a mesh: fine: 32 (over z, x, core), coarse: 4 (over y).
Axes of the slice: x: 4, y: 4, z: 4, core: 2. Of those that a mesh axis runs over, the one named last changes fastest.
Arguments:
- loads: float32 [12, 256, 32, 256], P(None, 'fine', 'coarse'), may hold values from -6 to 6
- rotations: float32 [9, 256, 32, 256], P(None, 'fine', 'coarse'), may hold values from -1 to 1, as said below
- occupancy: int32 [256, 32, 256], P('fine', 'coarse'), may hold values 0 or 1
- element_matrix: float32 [24, 24], replicated, as said below
- line_inverse: bfloat16 [16, 128, 384, 384], P('coarse', 'fine')
Outputs:
- displacement: float32 [12, 256, 32, 256], P(None, 'fine', 'coarse')
- residual: float32 [12, 256, 32, 256], P(None, 'fine', 'coarse')
Inputs may be any that keep to these rules, and one draw needn't show every extreme that they name: `rotations`: each element's nine entries form a rotation matrix. `element_matrix`: symmetric positive definite.
All inputs are finite; a program needn't handle non-finite values. No bound on the sum of `occupancy` on one device may be relied on, other than what follows from the above.
Results may differ from a plain program's by a relative error of at most 0.0041.
Values may be sent and summed in bfloat16 or wider, within the bound.
No kernel may reach another device: no remote copies, remote signals or barrier semaphores. Data moves between devices by JAX's collectives and lax.ppermute only.
A program may use at most 128 MiB of HBM per device.

v0:
```python
import functools

import jax
import jax.numpy as jnp
import ml_dtypes
import numpy as np
from jax import lax
from jax.experimental import pallas as pl
from jax.experimental.pallas import tpu as pltpu
from jax.sharding import PartitionSpec as P

relax_step = 0.1
spring = 0.1
bf16 = jnp.bfloat16
f32 = jnp.float32
FINE = 32
COARSE = 4


def swaps(count, first):
    target = list(range(count))
    for i in range(first, count - 1, 2):
        target[i], target[i + 1] = i + 1, i
    return [(i, target[i]) for i in range(count)]


def tables():
    n = np.arange(384)
    n_i, n_f, n_x = n // 128, n % 128 // 4, n % 4
    r = np.arange(128)
    r_x, r_y = r % 16 // 8 * 2 + r % 2, r % 8 // 2
    slots = np.arange(32)
    rows = np.arange(256)
    z = np.arange(256)
    spread = n_f[:, None] == slots[None]
    keep, fold, lift = [], [], []
    for half in range(2):
        r_q = r // 16 + 6 * half
        keep.append((r[None] < 96) & (n_i[:, None] == r_q[None] // 4) & (n_x[:, None] == r_x[None]))
        for zz in range(4):
            to = r_y * 16 + zz * 4 + r_q % 4
            fold.append((r[:, None] < 96) & (to[:, None] == r[None]))
        mine = rows[:, None] % 8 // 4 == half
        lift.append(mine & (rows[:, None] // 8 * 4 + rows[:, None] % 4 == z[None] // 2))
    d_q, d_x, d_y = n // 32, n % 32 // 8, n % 8 // 2
    grown = (d_q[:, None] % 6 == r[None] // 16) & (d_x[:, None] == r_x[None]) & (d_y[:, None] == r_y[None])
    as_bf16 = lambda a: np.asarray(a, np.float32).astype(ml_dtypes.bfloat16)
    return {
        "spread": as_bf16(spread),
        "gather": as_bf16(spread.T),
        "keep": as_bf16(np.stack(keep)),
        "fold": as_bf16(np.stack(fold)),
        "lift": as_bf16(np.stack(lift)),
        "grown": as_bf16(grown),
    }


def rooted(occupancy):
    return jnp.sqrt(0.02 + 0.98 * occupancy.astype(f32))


def row_index():
    return lax.broadcasted_iota(jnp.int32, (8, 256), 0)


def next_z(v):
    lane = lax.broadcasted_iota(jnp.int32, v.shape, 1)
    return jnp.where(lane == 255, 0.0, pltpu.roll(v, 255, 1))


def past_z(v):
    lane = lax.broadcasted_iota(jnp.int32, v.shape, 1)
    return jnp.where(lane == 0, 0.0, pltpu.roll(v, 1, 1))


def x_faces_kernel(
    loads_ref, rot_ref, occ_ref, matrix_ref, one_ref, two_ref, loads_out, rot_out, occ_out, matrix_out, arrived
):
    face = [
        pltpu.make_async_copy(loads_ref.at[:, 0], loads_out.at[:, 0], arrived.at[0]),
        pltpu.make_async_copy(loads_ref.at[:, 7], loads_out.at[:, 7], arrived.at[1]),
        pltpu.make_async_copy(rot_ref.at[:, 7], rot_out.at[:, 7], arrived.at[2]),
        pltpu.make_async_copy(occ_ref, occ_out, arrived.at[3]),
    ]
    rest = [
        pltpu.make_async_copy(loads_ref.at[:, 1:7], loads_out.at[:, 1:7], arrived.at[4]),
        pltpu.make_async_copy(rot_ref.at[:, 0:7], rot_out.at[:, 0:7], arrived.at[5]),
        pltpu.make_async_copy(matrix_ref, matrix_out, arrived.at[6]),
    ]
    for copy in face + rest:
        copy.start()
    even = lax.axis_index("fine") % 2 == 0
    for copy in face:
        copy.wait()
    weight = rooted(occ_out[7])
    for q in range(12):
        low, high = loads_out[q, 0], loads_out[q, 7]
        one_ref[q] = jnp.where(even, high, low).astype(bf16)
        two_ref[q] = jnp.where(even, low, high).astype(bf16)
    for k in range(9):
        scaled = (rot_out[k, 7] * weight).astype(bf16)
        one_ref[12 + k] = scaled
        two_ref[12 + k] = scaled
    for copy in rest:
        copy.wait()


def x_sides(one_ref, two_ref, k):
    place = lax.axis_index("fine")
    even = place % 2 == 0
    one, two = one_ref[k].astype(f32), two_ref[k].astype(f32)
    low = jnp.where(place == 0, 0.0, jnp.where(even, two, one))
    high = jnp.where(place == FINE - 1, 0.0, jnp.where(even, one, two))
    return low, high


def rows_kernel(loads_ref, rot_ref, occ_ref, matrix_ref, first_ref, last_ref, stiff_ref):
    zero = jnp.zeros((1, 256), f32)
    zeros = jnp.zeros((7, 256), f32)
    occ = [rooted(occ_ref[x]) for x in range(8)]
    for q in range(12):
        planes = [loads_ref[q, x] for x in range(8)]
        first_ref[q] = jnp.concatenate([zero] + [p[0:1] for p in planes] + [zeros], 0)
        last_ref[q] = jnp.concatenate([zero] + [p[7:8] for p in planes] + [zeros], 0)
    for k in range(9):
        planes = [rot_ref[k, x] * occ[x] for x in range(8)]
        last_ref[12 + k] = jnp.concatenate([zero] + [p[7:8] for p in planes] + [zeros], 0)
    tall = lax.broadcasted_iota(jnp.int32, (192, 24), 0) // 8
    copy = (tall == lax.broadcasted_iota(jnp.int32, (192, 24), 1)).astype(bf16)
    same = lax.broadcasted_iota(jnp.int32, (192, 192), 0) % 8
    same = same == lax.broadcasted_iota(jnp.int32, (192, 192), 1) % 8
    whole_matrix = matrix_ref[...]
    main = whole_matrix.astype(bf16)
    rest = (whole_matrix - main.astype(f32)).astype(bf16)
    for slot, part in ((0, main), (1, rest)):
        wide = jnp.dot(copy, part, preferred_element_type=f32).astype(bf16)
        wide = lax.dot_general(wide, copy, (((1,), (1,)), ((), ())), preferred_element_type=f32)
        stiff_ref[slot] = jnp.where(same, wide, 0.0).astype(bf16)


def y_faces_kernel(first_ref, last_ref, px1_ref, px2_ref, one_ref, two_ref, near_ref, far_ref):
    even = lax.axis_index("coarse") % 2 == 0
    row = lax.broadcasted_iota(jnp.int32, (16, 256), 0)

    def ends(own, low, high):
        return jnp.where(row == 0, low, jnp.where(row == 9, high, own))

    for q in range(12):
        low, high = x_sides(px1_ref, px2_ref, q)
        first = ends(first_ref[q], low[0:1], high[0:1])
        last = ends(last_ref[q], low[7:8], high[7:8])
        near_ref[q] = first
        one_ref[q] = jnp.where(even, last, first).astype(bf16)
        two_ref[q] = jnp.where(even, first, last).astype(bf16)
    for k in range(9):
        low, _ = x_sides(px1_ref, px2_ref, 12 + k)
        last = jnp.where(row == 0, low[7:8], last_ref[12 + k])
        far_ref[k] = last
        one_ref[12 + k] = last.astype(bf16)
        two_ref[12 + k] = last.astype(bf16)


def turn_in(scale, nodes):
    return [
        scale[i] * nodes[0] + scale[3 + i] * nodes[1] + scale[6 + i] * nodes[2] for i in range(3)
    ]


def turn_out(scale, forces):
    return [
        scale[3 * i] * forces[0] + scale[3 * i + 1] * forces[1] + scale[3 * i + 2] * forces[2]
        for i in range(3)
    ]


def element_forces(stiff_ref, local, scale, pick):
    held, at = [], 0
    for corner in range(8):
        got = pick(corner)
        held += [jnp.zeros((8, 256), f32)] * 3 if got is None else turn_in(scale, got)
        while len(held) >= 2:
            pair = jnp.concatenate(held[:2], 0)
            main = pair.astype(bf16)
            local[0, 16 * at : 16 * at + 16] = main
            local[1, 16 * at : 16 * at + 16] = (pair - main.astype(f32)).astype(bf16)
            held, at = held[2:], at + 1
    main, rest = stiff_ref[0], stiff_ref[1]
    out = jnp.dot(main, local[0], preferred_element_type=f32)
    out = out + jnp.dot(rest, local[0], preferred_element_type=f32)
    return out + jnp.dot(main, local[1], preferred_element_type=f32)


def corner_rows(out, corner):
    return [out[8 * (3 * corner + j) : 8 * (3 * corner + j) + 8] for j in range(3)]


def put_nodes(nodes, p, q, v):
    up = jnp.where(row_index() == 7, 0.0, pltpu.roll(v, 7, 0))
    nodes[p, 0, q] = v
    nodes[p, 1, q] = up
    nodes[p, 2, q] = next_z(v)
    nodes[p, 3, q] = next_z(up)


def settle(sides):
    own = sides[0] + past_z(sides[2])
    upper = sides[1] + past_z(sides[3])
    return own + jnp.where(row_index() == 0, 0.0, pltpu.roll(upper, 1, 0))


def picker(nodes, p, case):
    def pick(corner):
        off_x, off_y, off_z = corner % 2, corner // 2 % 2, corner // 4
        return [nodes[p + off_x, off_y + 2 * off_z, j * 4 + case] for j in range(3)]

    return pick


def inner_kernel(start, count, loads_ref, rot_ref, occ_ref, stiff_ref, force_ref, nodes, carry, local):
    @pl.loop(0, count + 1)
    def _(p):
        for q in range(12):
            put_nodes(nodes, p, q, loads_ref[q, start + p])

    carry[...] = jnp.zeros_like(carry)

    @pl.loop(0, count)
    def _(e):
        weight = rooted(occ_ref[start + e])
        scale = [rot_ref[k, start + e] * weight for k in range(9)]
        for case in range(4):
            out = element_forces(stiff_ref, local.at[case], scale, picker(nodes, e, case))
            total = [[None] * 4 for _ in range(3)]
            for corner in range(8):
                turned = turn_out(scale, corner_rows(out, corner))
                for i in range(3):
                    q = i * 4 + case
                    if corner % 2 == 0:
                        total[i][corner // 2] = turned[i] + carry[corner // 2, q]
                    else:
                        carry[corner // 2, q] = turned[i]
            for i in range(3):
                force_ref[i * 4 + case, e] = settle(total[i])

    for q in range(12):
        force_ref[q, count] = settle([carry[side, q] for side in range(4)])


def x_edges_kernel(
    low_ref, high_ref, rot_ref, occ_ref, px1_ref, px2_ref, stiff_ref, force_ref, nodes, scales, local
):
    weight = rooted(occ_ref[0])
    for q in range(12):
        low, high = x_sides(px1_ref, px2_ref, q)
        for p, v in enumerate((low, low_ref[q, 0], high_ref[q, 0], high)):
            put_nodes(nodes, p, q, v)
    for k in range(9):
        low, _ = x_sides(px1_ref, px2_ref, 12 + k)
        scales[0, k] = low
        scales[1, k] = rot_ref[k, 0] * weight
    for edge in range(2):
        scale = [scales[edge, k] for k in range(9)]
        for case in range(4):
            at = 4 * edge + case
            out = element_forces(stiff_ref, local.at[at], scale, picker(nodes, 2 * edge, case))
            sides = [turn_out(scale, corner_rows(out, 2 * side + 1 - edge)) for side in range(4)]
            for i in range(3):
                force_ref[edge, i * 4 + case] = settle([side[i] for side in sides])


def finish_kernel(
    loads_ref,
    py1_ref,
    py2_ref,
    near_ref,
    far_ref,
    stiff_ref,
    lift_ref,
    inner1_ref,
    inner2_ref,
    edges_ref,
    residual_ref,
    coarse_ref,
    below,
    above,
    low0,
    low1,
    high0,
    high1,
    ends,
    made,
    local,
    sums,
    sent,
):
    row = row_index()
    place = lax.axis_index("coarse")
    even = place % 2 == 0
    for k in range(21):
        one, two = py1_ref[k].astype(f32), py2_ref[k].astype(f32)
        below[k] = jnp.where(place == 0, 0.0, jnp.where(even, two, one))
        if k < 12:
            above[k] = jnp.where(place == COARSE - 1, 0.0, jnp.where(even, one, two))

    for upper in range(2):
        scale = [far_ref[k, 0:8] if upper else below[12 + k, 0:8] for k in range(9)]
        for case in range(4):

            def pick(corner):
                off_x, off_y, off_z = corner % 2, corner // 2 % 2, corner // 4
                if upper and not off_y:
                    return None
                source = above if upper else near_ref if off_y else below
                got = [source[j * 4 + case, off_x : off_x + 8] for j in range(3)]
                return [next_z(v) for v in got] if off_z else got

            out = element_forces(stiff_ref, local.at[4 * upper + case], scale, pick)
            for off_x, target in ((0, (low0, high0)[upper]), (1, (low1, high1)[upper])):
                flat = turn_out(scale, corner_rows(out, off_x + 2 - 2 * upper))
                tall = turn_out(scale, corner_rows(out, off_x + 6 - 2 * upper))
                for i in range(3):
                    target[i * 4 + case] = flat[i] + past_z(tall[i])

    lower = row < 4
    scale = [jnp.where(lower, below[12 + k, 8:9], far_ref[k, 8:9]) for k in range(9)]

    def pick_last(corner):
        off_x, off_y, off_z = corner % 2, corner // 2 % 2, corner // 4
        at = 8 + off_x
        got = []
        for j in range(3):
            source = near_ref if off_y else below
            rows = [source[j * 4 + case, at : at + 1] for case in range(4)]
            if off_y:
                rows += [above[j * 4 + case, at : at + 1] for case in range(4)]
            else:
                rows += [jnp.zeros((4, 256), f32)]
            got.append(jnp.concatenate(rows, 0))
        return [next_z(v) for v in got] if off_z else got

    out = element_forces(stiff_ref, local.at[8], scale, pick_last)
    flat = [jnp.where(lower, u, v) for u, v in zip(corner_rows(out, 2), corner_rows(out, 0))]
    tall = [jnp.where(lower, u, v) for u, v in zip(corner_rows(out, 6), corner_rows(out, 4))]
    flat, tall = turn_out(scale, flat), turn_out(scale, tall)
    for i in range(3):
        ends[i] = flat[i] + past_z(tall[i])

    def residual_of(q, x, force):
        if x < 7:
            first, last = low0[q, x + 1 : x + 2], high0[q, x + 1 : x + 2]
        else:
            case = q % 4
            first, last = ends[q // 4, case : case + 1], ends[q // 4, 4 + case : 5 + case]
        first = first + low1[q, x : x + 1]
        last = last + high1[q, x : x + 1]
        force = force + jnp.where(row == 0, first, 0.0) + jnp.where(row == 7, last, 0.0)
        given = loads_ref[q, x]
        left = given - relax_step * (spring * given + force)
        made[q, x] = left
        return left

    split = inner1_ref.shape[1] - 1
    copies = [pltpu.make_async_copy(made.at[q], residual_ref.at[q], sent.at[q]) for q in range(12)]
    for q in range(12):
        planes = []
        for x in range(8):
            force = inner1_ref[q, x] if x <= split else inner2_ref[q, x - split]
            if x == split:
                force = force + inner2_ref[q, 0]
            if x in (0, 7):
                force = force + edges_ref[x // 7, q]
            planes.append(residual_of(q, x, force))
        copies[q].start()
        for half in range(2):
            s0 = planes[4 * half] + planes[4 * half + 1]
            s1 = planes[4 * half + 2] + planes[4 * half + 3]
            t0 = s0 + pltpu.roll(s0, 7, 0)
            t1 = s1 + pltpu.roll(s1, 1, 0)
            at = 16 * (q % 6) + 8 * half
            sums[q // 6, at : at + 8] = jnp.where(row % 2 == 0, t0, t1)
    nt = (((1,), (1,)), ((), ()))
    coarse = None
    for half in range(2):
        sums[half, 96:128] = jnp.zeros((32, 256), f32)
        every = sums[half]
        main = every.astype(bf16)
        rest = (every - main.astype(f32)).astype(bf16)
        for part in (main, rest):
            term = lax.dot_general(lift_ref[half], part, nt, preferred_element_type=f32)
            coarse = term if coarse is None else coarse + term
    coarse_ref[...] = coarse.astype(bf16)
    for copy in copies:
        copy.wait()


def lines_kernel(
    got_ref, inverse_ref, spread_ref, gather_ref, keep_ref, fold_ref, sent_ref, rows, back
):
    nt = (((1,), (1,)), ((), ()))
    rows[...] = got_ref[...].astype(f32)
    vectors = jnp.zeros((384, 128), f32)
    for half in range(2):
        keep = keep_ref[half].astype(f32)
        for zz in range(4):
            part = rows[pl.ds(4 * half + zz, 32, stride=8), :].astype(bf16)
            wide = jnp.dot(spread_ref[...], part, preferred_element_type=f32) * keep
            fold = fold_ref[4 * half + zz]
            vectors = vectors + jnp.dot(wide.astype(bf16), fold, preferred_element_type=f32)
    vectors = vectors.astype(bf16)
    line = lax.broadcasted_iota(jnp.int32, (384, 128), 1) // 4
    solved = jnp.zeros((384, 128), f32)
    for k in range(16):
        one = jnp.dot(inverse_ref[k], vectors, preferred_element_type=f32)
        solved = jnp.where(line == k, one, solved)
    solved = solved.astype(bf16)
    for half in range(2):
        keep = keep_ref[half].astype(f32)
        for zz in range(4):
            fold = fold_ref[4 * half + zz]
            wide = lax.dot_general(solved, fold, nt, preferred_element_type=f32) * keep
            back[pl.ds(4 * half + zz, 32, stride=8), :] = jnp.dot(
                gather_ref[...], wide.astype(bf16), preferred_element_type=f32
            )
    sent_ref[...] = back[...].astype(bf16)


def correct_kernel(loads_ref, back_ref, grown_ref, lift_ref, out_ref, made, sent):
    nt = (((1,), (1,)), ((), ()))
    copies = [pltpu.make_async_copy(made.at[q], out_ref.at[q], sent.at[q]) for q in range(12)]
    tall = lax.dot_general(grown_ref[...], back_ref[...], nt, preferred_element_type=f32).astype(bf16)
    for half in range(2):
        mine = tall[192 * half : 192 * half + 192]
        coarse = jnp.dot(mine, lift_ref[half], preferred_element_type=f32)
        for q in range(6 * half, 6 * half + 6):
            for part in range(4):
                at = 32 * (q % 6) + 8 * part
                added = coarse[at : at + 8]
                for x in (2 * part, 2 * part + 1):
                    made[q, x] = relax_step * loads_ref[q, x] + added
            copies[q].start()
    for copy in copies:
        copy.wait()


def whole(count):
    return [pl.BlockSpec(memory_space=pltpu.VMEM)] * count


def params(mib):
    return pltpu.CompilerParams(vmem_limit_bytes=mib << 20)


def cost(us):
    return pl.CostEstimate(flops=0, bytes_accessed=int(us * 3.0e6), transcendentals=0)


def body(loads, rotations, occupancy, element_matrix, line_inverse):
    table = {name: jnp.asarray(value) for name, value in tables().items()}
    shape = jax.ShapeDtypeStruct
    face = shape((21, 8, 256), bf16)
    plane = lambda count, at: pl.BlockSpec((count, 1, 8, 256), lambda i: (0, at, 0, 0))
    px1, px2, loads, rotations, occupancy, matrix = pl.pallas_call(
        x_faces_kernel,
        in_specs=[pl.BlockSpec(memory_space=pltpu.MemorySpace.HBM)] * 4,
        out_specs=whole(6),
        out_shape=(
            face,
            face,
            shape(loads.shape, f32),
            shape(rotations.shape, f32),
            shape(occupancy.shape, jnp.int32),
            shape((24, 24), f32),
        ),
        scratch_shapes=[pltpu.SemaphoreType.DMA((7,))],
        compiler_params=pltpu.CompilerParams(vmem_limit_bytes=FIRST),
        name="x_faces",
    )(*(pltpu.with_memory_space_constraint(a, pltpu.MemorySpace.HBM) for a in (loads, rotations, occupancy, element_matrix)))
    px1 = lax.ppermute(px1, "fine", swaps(FINE, 0))
    px2 = lax.ppermute(px2, "fine", swaps(FINE, 1))
    first, last, stiff = pl.pallas_call(
        rows_kernel,
        in_specs=whole(4),
        out_specs=whole(3),
        out_shape=(shape((12, 16, 256), f32), shape((21, 16, 256), f32), shape((2, 192, 192), bf16)),
        compiler_params=params(8),
        cost_estimate=cost(2),
        name="rows",
    )(loads, rotations, occupancy, matrix)

    def inner(start, count):
        return pl.pallas_call(
            functools.partial(inner_kernel, start, count),
            in_specs=whole(4),
            out_specs=whole(1)[0],
            out_shape=shape((12, count + 1, 8, 256), f32),
            scratch_shapes=[
                pltpu.VMEM((count + 1, 4, 12, 8, 256), f32),
                pltpu.VMEM((4, 12, 8, 256), f32),
                pltpu.VMEM((4, 2, 192, 256), bf16),
            ],
            compiler_params=params(12),
            cost_estimate=cost(0.8 * count),
            name=f"inner_{start}",
        )(loads, rotations, occupancy, stiff)

    inner1 = inner(0, SPLIT)
    first, inner1 = lax.optimization_barrier((first, inner1))
    face = shape((21, 16, 256), bf16)
    py1, py2, near, far = pl.pallas_call(
        y_faces_kernel,
        in_specs=whole(4),
        out_specs=whole(4),
        out_shape=(face, face, shape((12, 16, 256), f32), shape((9, 16, 256), f32)),
        compiler_params=params(8),
        name="y_faces",
    )(first, last, px1, px2)
    py1 = lax.ppermute(py1, "coarse", swaps(COARSE, 0))
    py2 = lax.ppermute(py2, "coarse", swaps(COARSE, 1))
    inner2 = inner(SPLIT, 7 - SPLIT)
    edges = pl.pallas_call(
        x_edges_kernel,
        grid=(1,),
        in_specs=[
            plane(12, 0),
            plane(12, 7),
            plane(9, 7),
            pl.BlockSpec((1, 8, 256), lambda i: (7, 0, 0)),
            pl.BlockSpec((21, 8, 256), lambda i: (0, 0, 0)),
            pl.BlockSpec((21, 8, 256), lambda i: (0, 0, 0)),
            pl.BlockSpec((2, 192, 192), lambda i: (0, 0, 0)),
        ],
        out_specs=pl.BlockSpec((2, 12, 8, 256), lambda i: (0, 0, 0, 0)),
        out_shape=shape((2, 12, 8, 256), f32),
        scratch_shapes=[
            pltpu.VMEM((4, 4, 12, 8, 256), f32),
            pltpu.VMEM((2, 9, 8, 256), f32),
            pltpu.VMEM((8, 2, 192, 256), bf16),
        ],
        compiler_params=params(12),
        cost_estimate=cost(1.6),
        name="x_edges",
    )(loads, loads, rotations, occupancy, px1, px2, stiff)
    tall = lambda count, rows: pltpu.VMEM((count, rows, 256), f32)
    residual, coarse = pl.pallas_call(
        finish_kernel,
        in_specs=whole(10),
        out_specs=[pl.BlockSpec(memory_space=pltpu.MemorySpace.HBM)] + whole(1),
        out_shape=(shape((12, 8, 8, 256), f32), shape((256, 128), bf16)),
        scratch_shapes=[
            tall(21, 16), tall(12, 16),
            tall(12, 8), tall(12, 8), tall(12, 8), tall(12, 8), tall(3, 8),
            pltpu.VMEM((12, 8, 8, 256), f32),
            pltpu.VMEM((9, 2, 192, 256), bf16),
            tall(2, 128),
            pltpu.SemaphoreType.DMA((12,)),
        ],
        compiler_params=params(16),
        name="finish",
    )(loads, py1, py2, near, far, stiff, table["lift"], inner1, inner2, edges)
    got = lax.all_to_all(coarse.reshape(32, 8, 128), "fine", 0, 0, tiled=True)
    sent = pl.pallas_call(
        lines_kernel,
        in_specs=whole(6),
        out_specs=whole(1)[0],
        out_shape=shape((256, 128), bf16),
        scratch_shapes=[
            pltpu.VMEM((256, 128), f32),
            pltpu.VMEM((256, 128), f32),
        ],
        compiler_params=params(16),
        name="lines",
    )(
        got.reshape(256, 128),
        line_inverse.reshape(16, 384, 384),
        *(table[k] for k in ("spread", "gather", "keep", "fold")),
    )
    back = lax.all_to_all(sent.reshape(32, 8, 128), "fine", 0, 0, tiled=True)
    displacement = pl.pallas_call(
        correct_kernel,
        in_specs=whole(4),
        out_specs=pl.BlockSpec(memory_space=pltpu.MemorySpace.HBM),
        out_shape=shape((12, 8, 8, 256), f32),
        scratch_shapes=[pltpu.VMEM((12, 8, 8, 256), f32), pltpu.SemaphoreType.DMA((12,))],
        compiler_params=params(12),
        name="correct",
    )(loads, back.reshape(256, 128), table["grown"], table["lift"])
    return displacement, residual


SPLIT = 3
FIRST = 8 << 20

def solution(mesh):
    in_specs = (
        P(None, "fine", "coarse", None),
        P(None, "fine", "coarse", None),
        P("fine", "coarse", None),
        P(),
        P("coarse", "fine", None, None),
    )
    out_specs = (P(None, "fine", "coarse", None), P(None, "fine", "coarse", None))
    return jax.shard_map(body, mesh=mesh, in_specs=in_specs, out_specs=out_specs, check_vma=False)
```

profile of v0, /device:TPU:9, one launch (start us, length us, event | category | flops | bytes accessed | tf_op | source)
XLA Modules:
  0.0 52.5 jit_solution(5153904029230588932)
XLA Ops:
  0.6 1.5 %x_faces.1 = (bf16[21,8,256]{2,1,0:T(8,128)(2,1)S(1)}, bf16[21,8,256]{2,1,0:T(8,128)(2,1)S(1)}, f32[12,8,8,256]{3,2,1,0:T(8,128)S(1)}, f32[9,8,8,256]{3,2,1,0:T(...) custom-call(f32[12,8,8,256]{3,2,1,0:T(8,128)} %loads_ref.1, f32[9,8,8,256]{3,2,1,0:T(8,128)} %rot_ref.1, ...), custom_call_target="tpu_custom_call" | custom-call | tf_op jit(solution)/shard_map/x_faces/pallas_call | solution.py:462
  2.1 0.0 copy-start
  2.1 0.8 %collective-permute-start = (bf16[21,8,256]{2,1,0:T(8,128)(2,1)S(1)}, bf16[21,8,256]{2,1,0:T(8,128)(2,1)S(1)}, u32[]{:S(2)}, u32[]{:S(2)}) collective-permute-start(bf16[21,8,256]{2,1,0:T(8,128)(2,1)S(1)} %get-tuple-element.27), channel_id=1, source_target_pairs={{0,4},{4,0},{8,12},{12,8},{16,20},{20,16},{24,28},{28,24},{32,36},... | collective-permute-start | bytes 258056 | tf_op jit(solution)/shard_map/ppermute | solution.py:478
  2.9 3.0 %collective-permute-start.1 = (bf16[21,8,256]{2,1,0:T(8,128)(2,1)S(1)}, bf16[21,8,256]{2,1,0:T(8,128)(2,1)S(1)}, u32[]{:S(2)}, u32[]{:S(2)}) collective-permute-start(bf16[21,8,256]{2,1,0:T(8,128)(2,1)S(1)} %get-tuple-element.28), channel_id=1, source_target_pairs={{0,0},{4,8},{8,4},{12,16},{16,12},{20,24},{24,20},{28,32},{32,28},... | collective-permute-start | bytes 258056 | tf_op jit(solution)/shard_map/ppermute | solution.py:479
  5.9 0.0 slice-start
  5.9 0.5 rows.1
  6.4 2.6 %inner_0.1.inner1_ref = f32[12,4,8,256]{3,2,1,0:T(8,128)S(1)} custom-call(f32[12,8,8,256]{3,2,1,0:T(8,128)S(1)} %get-tuple-element.19.loads_ref.low_ref.high_ref, f32[9,8,8,256]{3,2,1,0:T(8,128)S(1)} %get-tuple-element.20.rot_ref, s32[8,8,256]{2,1,0:T(8,128)S(1)} %get-tuple-element.21.occ_ref, bf16[2,192,192]{2,1,0:T(8,128)(2,1)S(1)} %get-tuple-element.24.stiff_ref), custom_call_target="tpu_custom_call" | custom-call | bytes 7200000 | tf_op jit(solution)/shard_map/inner_0/pallas_call | solution.py:491
  9.0 0.0 copy-start.1
  9.0 0.0 copy-start.2
  9.0 0.0 copy-start.4
  9.0 0.0 copy-start.5
  9.0 0.0 collective-permute-done.px1_ref
  9.0 0.0 collective-permute-done.1.px2_ref
  9.0 0.1 y_faces.1
  9.2 0.3 collective-permute-start.2
  9.4 0.0 slice-start.1
  9.4 4.2 %collective-permute-start.3 = (bf16[21,16,256]{2,1,0:T(8,128)(2,1)S(1)}, bf16[21,16,256]{2,1,0:T(8,128)(2,1)S(1)}, u32[]{:S(2)}, u32[]{:S(2)}) collective-permute-start(bf16[21,16,256]{2,1,0:T(8,128)(2,1)S(1)} %get-tuple-element.30), channel_id=1, source_target_pairs={{0,0},{1,2},{2,1},{3,3},{4,4},{5,6},{6,5},{7,7},{8,8},{9,10},{10,9... | collective-permute-start | bytes 516104 | tf_op jit(solution)/shard_map/ppermute | solution.py:518
  13.6 3.4 %inner_3.1.inner2_ref = f32[12,5,8,256]{3,2,1,0:T(8,128)S(1)} custom-call(f32[12,8,8,256]{3,2,1,0:T(8,128)S(1)} %get-tuple-element.19.loads_ref.low_ref.high_ref, f32[9,8,8,256]{3,2,1,0:T(8,128)S(1)} %get-tuple-element.20.rot_ref, s32[8,8,256]{2,1,0:T(8,128)S(1)} %get-tuple-element.21.occ_ref, bf16[2,192,192]{2,1,0:T(8,128)(2,1)S(1)} %get-tuple-element.24.stiff_ref), custom_call_target="tpu_custom_call" | custom-call | bytes 9600000 | tf_op jit(solution)/shard_map/inner_3/pallas_call | solution.py:491
  16.9 1.1 %x_edges.1.edges_ref = f32[2,12,8,256]{3,2,1,0:T(8,128)S(1)} custom-call(f32[12,8,8,256]{3,2,1,0:T(8,128)S(1)} %get-tuple-element.19.loads_ref.low_ref.high_ref, f32[12,8,8,256]{3,2,1,0:T(8,128)S(1)} %get-tuple-element.19.loads_ref.low_ref.high_ref, f32[9,8,8,256]{3,2,1,0:T(8,128)S(1)} %get-tuple-element.20.rot_ref, ...), custom_call_target="tpu_custom_call" | custom-call | bytes 4800000 | tf_op jit(solution)/shard_map/x_edges/pallas_call | solution.py:520
  18.1 0.0 copy-start.3
  18.1 0.0 collective-permute-done.2.py1_ref
  18.1 0.0 collective-permute-done.3.py2_ref
  18.1 0.0 copy-done
  18.1 2.4 %finish.1 = (f32[12,8,8,256]{3,2,1,0:T(8,128)}, bf16[256,128]{1,0:T(8,128)(2,1)S(1)}) custom-call(f32[12,8,8,256]{3,2,1,0:T(8,128)S(1)} %get-tuple-element.19.loads_ref.low_ref.high_ref, bf16[21,16,256]{2,1,0:T(8,128)(2,1)S(1)} %collective-permute-done.2.py1_ref, bf16[21,16,256]{2,1,0:T(8,128)(2,1)S(1)} %collective-permute-done.3.py2_ref, ...), custom_call_target="tpu_custom_call" | custom-call | tf_op jit(solution)/shard_map/finish/pallas_call | solution.py:544
  20.5 16.5 %all_to_all.10 = bf16[32,8,128]{2,1,0:T(8,128)(2,1)S(1)} all-to-all(bf16[32,8,128]{2,1,0:T(8,128)(2,1)S(1)} %bitcast.11), channel_id=1, replica_groups=mesh['fine'=32,'coarse'=4] {'fine'}, dimensions={0} | all-to-all | bytes 131072 | tf_op jit(solution)/shard_map/all_to_all | solution.py:560
  37.0 0.0 slice-done
  37.0 0.0 copy-done.1
  37.0 0.0 copy-done.2
  37.0 0.0 copy-done.4
  37.0 0.0 copy-done.5
  37.0 0.0 slice-done.1
  37.0 3.3 %lines.1 = bf16[256,128]{1,0:T(8,128)(2,1)S(1)} custom-call(bf16[256,128]{1,0:T(8,128)(2,1)S(1)} %bitcast.8, bf16[16,384,384]{2,1,0:T(8,128)(2,1)S(1)} %bitcast.7, bf16[384,32]{1,0:T(8,128)(2,1)S(1)} %copy-done.4, bf16[32,384]{1,0:T(8,128)(2,1)S(1)} %copy-done.5, bf16[2,384,128]{2,1,0:T(8,128)(2,1)S(1)} %copy-done.2, bf16[8,128,128]{2,1,0:T(8,128)(2,1)S(1)} %copy-done.1), custom_call_target="tpu_custom_call" | custom-call | tf_op jit(solution)/shard_map/lines/pallas_call | solution.py:561
  40.4 10.9 %all_to_all.11 = bf16[32,8,128]{2,1,0:T(8,128)(2,1)S(1)} all-to-all(bf16[32,8,128]{2,1,0:T(8,128)(2,1)S(1)} %bitcast.9), channel_id=1, replica_groups=mesh['fine'=32,'coarse'=4] {'fine'}, dimensions={0} | all-to-all | bytes 131072 | tf_op jit(solution)/shard_map/all_to_all | solution.py:577
  51.2 0.0 copy-done.3
  51.2 1.2 %correct.1 = f32[12,8,8,256]{3,2,1,0:T(8,128)} custom-call(f32[12,8,8,256]{3,2,1,0:T(8,128)S(1)} %get-tuple-element.19.loads_ref.low_ref.high_ref, bf16[256,128]{1,0:T(8,128)(2,1)S(1)} %bitcast.10, bf16[384,128]{1,0:T(8,128)(2,1)S(1)} %copy-done.3, bf16[2,256,256]{2,1,0:T(8,128)(2,1)S(1)} %copy-done), custom_call_target="tpu_custom_call" | custom-call | tf_op jit(solution)/shard_map/correct/pallas_call | solution.py:578
  (1 shorter events, 0.0 us)
Async XLA Ops:
  2.1 16.0 %copy-start = (bf16[2,256,256]{2,1,0:T(8,128)(2,1)S(1)}, bf16[2,256,256]{2,1,0:T(8,128)(2,1)}, u32[]{:S(2)}) copy-start(bf16[2,256,256]{2,1,0:T(8,128)(2,1)} %constant.16.clone.lift_ref) | copy-start | bytes 786436
  2.1 6.9 %collective-permute-start = (bf16[21,8,256]{2,1,0:T(8,128)(2,1)S(1)}, bf16[21,8,256]{2,1,0:T(8,128)(2,1)S(1)}, u32[]{:S(2)}, u32[]{:S(2)}) collective-permute-start(bf16[21,8,256]{2,1,0:T(8,128)(2,1)S(1)} %get-tuple-element.27), channel_id=1, source_target_pairs={{0,4},{4,0},{8,12},{12,8},{16,20},{20,16},{24,28},{28,24},{32,36},... | collective-permute-start | bytes 258056 | tf_op jit(solution)/shard_map/ppermute | solution.py:478
  2.9 6.2 %collective-permute-start.1 = (bf16[21,8,256]{2,1,0:T(8,128)(2,1)S(1)}, bf16[21,8,256]{2,1,0:T(8,128)(2,1)S(1)}, u32[]{:S(2)}, u32[]{:S(2)}) collective-permute-start(bf16[21,8,256]{2,1,0:T(8,128)(2,1)S(1)} %get-tuple-element.28), channel_id=1, source_target_pairs={{0,0},{4,8},{8,4},{12,16},{16,12},{20,24},{24,20},{28,32},{32,28},... | collective-permute-start | bytes 258056 | tf_op jit(solution)/shard_map/ppermute | solution.py:479
  5.9 31.1 %slice-start = ((s8[4718592]{0:T(1024)(128)(4,1)}), s8[4194304]{0:T(1024)(128)(4,1)S(1)}, s32[]{:S(2)}) async-start(s8[4718592]{0:T(1024)(128)(4,1)} %bitcast.5), calls=%async_computation.2 | async-start | bytes 8388608
  9.0 28.0 %copy-start.1 = (bf16[8,128,128]{2,1,0:T(8,128)(2,1)S(1)}, bf16[8,128,128]{2,1,0:T(8,128)(2,1)}, u32[]{:S(2)}) copy-start(bf16[8,128,128]{2,1,0:T(8,128)(2,1)} %constant.15.clone.fold_ref) | copy-start | bytes 786436
  9.0 28.0 %copy-start.2 = (bf16[2,384,128]{2,1,0:T(8,128)(2,1)S(1)}, bf16[2,384,128]{2,1,0:T(8,128)(2,1)}, u32[]{:S(2)}) copy-start(bf16[2,384,128]{2,1,0:T(8,128)(2,1)} %constant.14.clone.keep_ref) | copy-start | bytes 589828
  9.0 28.0 %copy-start.4 = (bf16[384,32]{1,0:T(8,128)(2,1)S(1)}, bf16[384,32]{1,0:T(8,128)(2,1)}, u32[]{:S(2)}) copy-start(bf16[384,32]{1,0:T(8,128)(2,1)} %constant.12.clone.spread_ref) | copy-start | bytes 73732
  9.0 28.0 %copy-start.5 = (bf16[32,384]{1,0:T(8,128)(2,1)S(1)}, bf16[32,384]{1,0:T(8,128)(2,1)}, u32[]{:S(2)}) copy-start(bf16[32,384]{1,0:T(8,128)(2,1)} %constant.13.clone.gather_ref) | copy-start | bytes 73732
  9.2 8.9 %collective-permute-start.2 = (bf16[21,16,256]{2,1,0:T(8,128)(2,1)S(1)}, bf16[21,16,256]{2,1,0:T(8,128)(2,1)S(1)}, u32[]{:S(2)}, u32[]{:S(2)}) collective-permute-start(bf16[21,16,256]{2,1,0:T(8,128)(2,1)S(1)} %get-tuple-element.29), channel_id=1, source_target_pairs={{0,1},{1,0},{2,3},{3,2},{4,5},{5,4},{6,7},{7,6},{8,9},{9,8},{10,11... | collective-permute-start | bytes 516104 | tf_op jit(solution)/shard_map/ppermute | solution.py:517
  9.4 27.6 %slice-start.1 = ((s8[4718592]{0:T(1024)(128)(4,1)}), s8[524288]{0:T(1024)(128)(4,1)S(1)}, s32[]{:S(2)}) async-start(s8[4718592]{0:T(1024)(128)(4,1)} %bitcast.5), calls=%async_computation.3 | async-start | bytes 1048576
  9.4 8.7 %collective-permute-start.3 = (bf16[21,16,256]{2,1,0:T(8,128)(2,1)S(1)}, bf16[21,16,256]{2,1,0:T(8,128)(2,1)S(1)}, u32[]{:S(2)}, u32[]{:S(2)}) collective-permute-start(bf16[21,16,256]{2,1,0:T(8,128)(2,1)S(1)} %get-tuple-element.30), channel_id=1, source_target_pairs={{0,0},{1,2},{2,1},{3,3},{4,4},{5,6},{6,5},{7,7},{8,8},{9,10},{10,9... | collective-permute-start | bytes 516104 | tf_op jit(solution)/shard_map/ppermute | solution.py:518
  18.1 33.2 %copy-start.3 = (bf16[384,128]{1,0:T(8,128)(2,1)S(1)}, bf16[384,128]{1,0:T(8,128)(2,1)}, u32[]{:S(2)}) copy-start(bf16[384,128]{1,0:T(8,128)(2,1)} %constant.17.clone.grown_ref) | copy-start | bytes 294916
where the time goes:
time: 52.7 us; the launch traced here: 52.5 us
  blocking collectives  27.3 us (52%)
  Pallas kernels  16.1 us (31%)
  starting transfers between devices  8.18 us (16%)
  between operations  0.84 us (2%)
    all_to_all x1, blocking collectives, body(): got = lax.all_to_all(coarse.reshape(32, 8, 128), 'fine', 0, 0, tiled=True)  16.5 us
    all_to_all x1, blocking collectives, body(): back = lax.all_to_all(sent.reshape(32, 8, 128), 'fine', 0, 0, tiled=True)  10.9 us
    pallas_call x2, Pallas kernels, inner(): pl.pallas_call(functools.partial(inner_kernel, start, count), in_specs=wh...  5.93 us
    ppermute x1, starting transfers between devices, body(): py2 = lax.ppermute(py2, 'coarse', swaps(COARSE, 1))  4.15 us
    pallas_call x1, Pallas kernels, body(): pl.pallas_call(lines_kernel, in_specs=whole(6), out_specs=whole(1)[0], ou...  3.31 us
    ppermute x1, starting transfers between devices, body(): px2 = lax.ppermute(px2, 'fine', swaps(FINE, 1))  3.02 us
    pallas_call x1, Pallas kernels, body(): pl.pallas_call(finish_kernel, in_specs=whole(10), out_specs=[pl.BlockSpec...  2.4 us
    pallas_call x1, Pallas kernels, body(): pl.pallas_call(x_faces_kernel, in_specs=[pl.BlockSpec(memory_space=pltpu....  1.46 us
  transfers between devices with their start and end apart: 4, of which 0 were waited for; matrix products, arithmetic and copies ran while one was open for 0% of the time, Pallas kernels for 14%

commit v1 on v0

--- a/solution.py
+++ b/solution.py
@@ -49,7 +49,7 @@
         "spread": as_bf16(spread),
         "gather": as_bf16(spread.T),
         "keep": as_bf16(np.stack(keep)),
-        "fold": as_bf16(np.stack(fold)),
+        "fold": as_bf16(np.stack(fold).reshape(4, 256, 128)),
         "lift": as_bf16(np.stack(lift)),
         "grown": as_bf16(grown),
     }
@@ -115,16 +115,14 @@
 
 
 def rows_kernel(loads_ref, rot_ref, occ_ref, matrix_ref, first_ref, last_ref, stiff_ref):
-    zero = jnp.zeros((1, 256), f32)
-    zeros = jnp.zeros((7, 256), f32)
     occ = [rooted(occ_ref[x]) for x in range(8)]
     for q in range(12):
         planes = [loads_ref[q, x] for x in range(8)]
-        first_ref[q] = jnp.concatenate([zero] + [p[0:1] for p in planes] + [zeros], 0)
-        last_ref[q] = jnp.concatenate([zero] + [p[7:8] for p in planes] + [zeros], 0)
+        first_ref[q] = jnp.concatenate([p[0:1] for p in planes], 0)
+        last_ref[q] = jnp.concatenate([p[7:8] for p in planes], 0)
     for k in range(9):
         planes = [rot_ref[k, x] * occ[x] for x in range(8)]
-        last_ref[12 + k] = jnp.concatenate([zero] + [p[7:8] for p in planes] + [zeros], 0)
+        last_ref[12 + k] = jnp.concatenate([p[7:8] for p in planes], 0)
     tall = lax.broadcasted_iota(jnp.int32, (192, 24), 0) // 8
     copy = (tall == lax.broadcasted_iota(jnp.int32, (192, 24), 1)).astype(bf16)
     same = lax.broadcasted_iota(jnp.int32, (192, 192), 0) % 8
@@ -140,24 +138,29 @@
 
 def y_faces_kernel(first_ref, last_ref, px1_ref, px2_ref, one_ref, two_ref, near_ref, far_ref):
     even = lax.axis_index("coarse") % 2 == 0
-    row = lax.broadcasted_iota(jnp.int32, (16, 256), 0)
-
-    def ends(own, low, high):
-        return jnp.where(row == 0, low, jnp.where(row == 9, high, own))
-
-    for q in range(12):
-        low, high = x_sides(px1_ref, px2_ref, q)
-        first = ends(first_ref[q], low[0:1], high[0:1])
-        last = ends(last_ref[q], low[7:8], high[7:8])
-        near_ref[q] = first
-        one_ref[q] = jnp.where(even, last, first).astype(bf16)
-        two_ref[q] = jnp.where(even, first, last).astype(bf16)
-    for k in range(9):
-        low, _ = x_sides(px1_ref, px2_ref, 12 + k)
-        last = jnp.where(row == 0, low[7:8], last_ref[12 + k])
-        far_ref[k] = last
-        one_ref[12 + k] = last.astype(bf16)
-        two_ref[12 + k] = last.astype(bf16)
+    sides = [x_sides(px1_ref, px2_ref, k) for k in range(21)]
+
+    def column(side, count, row, rows):
+        picked = [sides[k][side][row : row + 1] for k in range(count)]
+        return jnp.concatenate(picked + [jnp.zeros((rows - count, 256), f32)], 0)
+
+    def send(tile, last, first):
+        one_ref[tile] = jnp.where(even, last, first).astype(bf16)
+        two_ref[tile] = jnp.where(even, first, last).astype(bf16)
+
+    for k in range(21):
+        last = last_ref[k]
+        send(k, last, first_ref[k] if k < 12 else last)
+    low_last = column(0, 21, 7, 24)
+    near_low, high_last, near_high = column(0, 12, 0, 16), column(1, 12, 7, 16), column(1, 12, 0, 16)
+    near_ref[0] = near_low
+    near_ref[1] = near_high
+    far_ref[...] = low_last[8:24]
+    for tile in range(2):
+        at = 8 * tile
+        send(21 + tile, low_last[at : at + 8], near_low[at : at + 8])
+        send(24 + tile, high_last[at : at + 8], near_high[at : at + 8])
+    send(23, low_last[16:24], low_last[16:24])
 
 
 def turn_in(scale, nodes):
@@ -270,6 +273,8 @@
 
 def finish_kernel(
     loads_ref,
+    first_ref,
+    last_ref,
     py1_ref,
     py2_ref,
     near_ref,
@@ -283,11 +288,8 @@
     coarse_ref,
     below,
     above,
-    low0,
-    low1,
-    high0,
-    high1,
-    ends,
+    low,
+    high,
     made,
     local,
     sums,
@@ -296,64 +298,76 @@
     row = row_index()
     place = lax.axis_index("coarse")
     even = place % 2 == 0
-    for k in range(21):
+    for k in range(26):
         one, two = py1_ref[k].astype(f32), py2_ref[k].astype(f32)
-        below[k] = jnp.where(place == 0, 0.0, jnp.where(even, two, one))
-        if k < 12:
-            above[k] = jnp.where(place == COARSE - 1, 0.0, jnp.where(even, one, two))
+        below[8 * k : 8 * k + 8] = jnp.where(place == 0, 0.0, jnp.where(even, two, one))
+        above[8 * k : 8 * k + 8] = jnp.where(place == COARSE - 1, 0.0, jnp.where(even, one, two))
+
+    def tile(source, k):
+        return source[8 * k : 8 * k + 8]
+
+    def single(source, at):
+        return source[at : at + 1]
+
+    lower = row < 4
+    scale = [jnp.where(lower, single(below, 180 + k), single(far_ref, 4 + k)) for k in range(9)]
+
+    def pick_first(corner):
+        off_x, off_y, off_z = corner % 2, corner // 2 % 2, corner // 4
+        got = []
+        for j in range(3):
+            rows = []
+            for case in range(4):
+                q = j * 4 + case
+                if off_y:
+                    rows.append(first_ref[q, 0:1] if off_x else near_ref[0, q : q + 1])
+                else:
+                    rows.append(single(below, 8 * q if off_x else 168 + q))
+            if off_y:
+                rows += [single(above, 8 * q if off_x else 168 + q) for q in range(4 * j, 4 * j + 4)]
+            else:
+                rows.append(jnp.zeros((4, 256), f32))
+            got.append(jnp.concatenate(rows, 0))
+        return [next_z(v) for v in got] if off_z else got
+
+    out = element_forces(stiff_ref, local.at[8], scale, pick_first)
+    flat = [jnp.where(lower, u, v) for u, v in zip(corner_rows(out, 3), corner_rows(out, 1))]
+    tall = [jnp.where(lower, u, v) for u, v in zip(corner_rows(out, 7), corner_rows(out, 5))]
+    flat, tall = turn_out(scale, flat), turn_out(scale, tall)
+    ends = [flat[i] + past_z(tall[i]) for i in range(3)]
 
     for upper in range(2):
-        scale = [far_ref[k, 0:8] if upper else below[12 + k, 0:8] for k in range(9)]
+        scale = [last_ref[12 + k] if upper else tile(below, 12 + k) for k in range(9)]
         for case in range(4):
 
             def pick(corner):
                 off_x, off_y, off_z = corner % 2, corner // 2 % 2, corner // 4
                 if upper and not off_y:
                     return None
-                source = above if upper else near_ref if off_y else below
-                got = [source[j * 4 + case, off_x : off_x + 8] for j in range(3)]
+                got = []
+                for q in (case, 4 + case, 8 + case):
+                    if not upper and off_y:
+                        v, past = first_ref[q], near_ref[1, q : q + 1]
+                    else:
+                        source = above if upper else below
+                        v, past = tile(source, q), single(source, 192 + q)
+                    got.append(jnp.where(row == 7, past, pltpu.roll(v, 7, 0)) if off_x else v)
                 return [next_z(v) for v in got] if off_z else got
 
             out = element_forces(stiff_ref, local.at[4 * upper + case], scale, pick)
-            for off_x, target in ((0, (low0, high0)[upper]), (1, (low1, high1)[upper])):
+            sides = []
+            for off_x in range(2):
                 flat = turn_out(scale, corner_rows(out, off_x + 2 - 2 * upper))
                 tall = turn_out(scale, corner_rows(out, off_x + 6 - 2 * upper))
-                for i in range(3):
-                    target[i * 4 + case] = flat[i] + past_z(tall[i])
-
-    lower = row < 4
-    scale = [jnp.where(lower, below[12 + k, 8:9], far_ref[k, 8:9]) for k in range(9)]
-
-    def pick_last(corner):
-        off_x, off_y, off_z = corner % 2, corner // 2 % 2, corner // 4
-        at = 8 + off_x
-        got = []
-        for j in range(3):
-            source = near_ref if off_y else below
-            rows = [source[j * 4 + case, at : at + 1] for case in range(4)]
-            if off_y:
-                rows += [above[j * 4 + case, at : at + 1] for case in range(4)]
-            else:
-                rows += [jnp.zeros((4, 256), f32)]
-            got.append(jnp.concatenate(rows, 0))
-        return [next_z(v) for v in got] if off_z else got
-
-    out = element_forces(stiff_ref, local.at[8], scale, pick_last)
-    flat = [jnp.where(lower, u, v) for u, v in zip(corner_rows(out, 2), corner_rows(out, 0))]
-    tall = [jnp.where(lower, u, v) for u, v in zip(corner_rows(out, 6), corner_rows(out, 4))]
-    flat, tall = turn_out(scale, flat), turn_out(scale, tall)
-    for i in range(3):
-        ends[i] = flat[i] + past_z(tall[i])
+                sides.append([flat[i] + past_z(tall[i]) for i in range(3)])
+            at = 4 * upper + case
+            for i in range(3):
+                past = jnp.where(row == 0, ends[i][at : at + 1], pltpu.roll(sides[1][i], 1, 0))
+                (low, high)[upper][i * 4 + case] = sides[0][i] + past
 
     def residual_of(q, x, force):
-        if x < 7:
-            first, last = low0[q, x + 1 : x + 2], high0[q, x + 1 : x + 2]
-        else:
-            case = q % 4
-            first, last = ends[q // 4, case : case + 1], ends[q // 4, 4 + case : 5 + case]
-        first = first + low1[q, x : x + 1]
-        last = last + high1[q, x : x + 1]
-        force = force + jnp.where(row == 0, first, 0.0) + jnp.where(row == 7, last, 0.0)
+        force = force + jnp.where(row == 0, low[q, x : x + 1], 0.0)
+        force = force + jnp.where(row == 7, high[q, x : x + 1], 0.0)
         given = loads_ref[q, x]
         left = given - relax_step * (spring * given + force)
         made[q, x] = left
@@ -401,11 +415,12 @@
     vectors = jnp.zeros((384, 128), f32)
     for half in range(2):
         keep = keep_ref[half].astype(f32)
-        for zz in range(4):
-            part = rows[pl.ds(4 * half + zz, 32, stride=8), :].astype(bf16)
+        keep = jnp.concatenate([keep, keep], 1)
+        for pair in range(2 * half, 2 * half + 2):
+            part = [rows[pl.ds(2 * pair + k, 32, stride=8), :] for k in range(2)]
+            part = jnp.concatenate(part, 1).astype(bf16)
             wide = jnp.dot(spread_ref[...], part, preferred_element_type=f32) * keep
-            fold = fold_ref[4 * half + zz]
-            vectors = vectors + jnp.dot(wide.astype(bf16), fold, preferred_element_type=f32)
+            vectors = vectors + jnp.dot(wide.astype(bf16), fold_ref[pair], preferred_element_type=f32)
     vectors = vectors.astype(bf16)
     line = lax.broadcasted_iota(jnp.int32, (384, 128), 1) // 4
     solved = jnp.zeros((384, 128), f32)
@@ -415,12 +430,12 @@
     solved = solved.astype(bf16)
     for half in range(2):
         keep = keep_ref[half].astype(f32)
-        for zz in range(4):
-            fold = fold_ref[4 * half + zz]
-            wide = lax.dot_general(solved, fold, nt, preferred_element_type=f32) * keep
-            back[pl.ds(4 * half + zz, 32, stride=8), :] = jnp.dot(
-                gather_ref[...], wide.astype(bf16), preferred_element_type=f32
-            )
+        keep = jnp.concatenate([keep, keep], 1)
+        for pair in range(2 * half, 2 * half + 2):
+            wide = lax.dot_general(solved, fold_ref[pair], nt, preferred_element_type=f32) * keep
+            part = jnp.dot(gather_ref[...], wide.astype(bf16), preferred_element_type=f32)
+            for k in range(2):
+                back[pl.ds(2 * pair + k, 32, stride=8), :] = part[:, 128 * k : 128 * k + 128]
     sent_ref[...] = back[...].astype(bf16)
 
 
@@ -481,7 +496,7 @@
         rows_kernel,
         in_specs=whole(4),
         out_specs=whole(3),
-        out_shape=(shape((12, 16, 256), f32), shape((21, 16, 256), f32), shape((2, 192, 192), bf16)),
+        out_shape=(shape((12, 8, 256), f32), shape((21, 8, 256), f32), shape((2, 192, 192), bf16)),
         compiler_params=params(8),
         cost_estimate=cost(2),
         name="rows",
@@ -505,12 +520,12 @@
 
     inner1 = inner(0, SPLIT)
     first, inner1 = lax.optimization_barrier((first, inner1))
-    face = shape((21, 16, 256), bf16)
+    face = shape((26, 8, 256), bf16)
     py1, py2, near, far = pl.pallas_call(
         y_faces_kernel,
         in_specs=whole(4),
         out_specs=whole(4),
-        out_shape=(face, face, shape((12, 16, 256), f32), shape((9, 16, 256), f32)),
+        out_shape=(face, face, shape((2, 16, 256), f32), shape((16, 256), f32)),
         compiler_params=params(8),
         name="y_faces",
     )(first, last, px1, px2)
@@ -540,23 +555,24 @@
         cost_estimate=cost(1.6),
         name="x_edges",
     )(loads, loads, rotations, occupancy, px1, px2, stiff)
-    tall = lambda count, rows: pltpu.VMEM((count, rows, 256), f32)
     residual, coarse = pl.pallas_call(
         finish_kernel,
-        in_specs=whole(10),
+        in_specs=whole(12),
         out_specs=[pl.BlockSpec(memory_space=pltpu.MemorySpace.HBM)] + whole(1),
         out_shape=(shape((12, 8, 8, 256), f32), shape((256, 128), bf16)),
         scratch_shapes=[
-            tall(21, 16), tall(12, 16),
-            tall(12, 8), tall(12, 8), tall(12, 8), tall(12, 8), tall(3, 8),
+            pltpu.VMEM((208, 256), f32),
+            pltpu.VMEM((208, 256), f32),
+            pltpu.VMEM((12, 8, 256), f32),
+            pltpu.VMEM((12, 8, 256), f32),
             pltpu.VMEM((12, 8, 8, 256), f32),
             pltpu.VMEM((9, 2, 192, 256), bf16),
-            tall(2, 128),
+            pltpu.VMEM((2, 128, 256), f32),
             pltpu.SemaphoreType.DMA((12,)),
         ],
         compiler_params=params(16),
         name="finish",
-    )(loads, py1, py2, near, far, stiff, table["lift"], inner1, inner2, edges)
+    )(loads, first, last, py1, py2, near, far, stiff, table["lift"], inner1, inner2, edges)
     got = lax.all_to_all(coarse.reshape(32, 8, 128), "fine", 0, 0, tiled=True)
     sent = pl.pallas_call(
         lines_kernel,
@@ -587,7 +603,7 @@
     return displacement, residual
 
 
-SPLIT = 3
+SPLIT = 4
 FIRST = 8 << 20
 
 def solution(mesh):

time: 52.7 us -> 51.6 us (0.979)
  blocking collectives: 27.3 us -> 26.6 us
    all_to_all x1, blocking collectives: 16.5 us -> 15.7 us  [body(): got = lax.all_to_all(coarse.reshape(32, 8, 128), 'fine', 0, 0, tiled=True)]
  transfers between devices with their start and end apart: 4 -> 4, of which waited for: 0 -> 0; matrix products, arithmetic and copies ran while one was open for 0% -> 0% of each run, Pallas kernels for 14% -> 15%
where the time goes in v1:
time: 51.6 us; the launch traced here: 51.4 us
  blocking collectives  26.6 us (52%)
  Pallas kernels  15.8 us (31%)
  starting transfers between devices  8.18 us (16%)
  between operations  0.84 us (2%)
    all_to_all x1, blocking collectives, body(): got = lax.all_to_all(coarse.reshape(32, 8, 128), 'fine', 0, 0, tiled=True)  15.7 us
    all_to_all x1, blocking collectives, body(): back = lax.all_to_all(sent.reshape(32, 8, 128), 'fine', 0, 0, tiled=True)  10.9 us
    pallas_call x2, Pallas kernels, inner(): pl.pallas_call(functools.partial(inner_kernel, start, count), in_specs=wh...  5.93 us
    ppermute x1, starting transfers between devices, body(): py2 = lax.ppermute(py2, 'coarse', swaps(COARSE, 1))  4.17 us
    pallas_call x1, Pallas kernels, body(): pl.pallas_call(lines_kernel, in_specs=whole(6), out_specs=whole(1)[0], ou...  3.17 us
    ppermute x1, starting transfers between devices, body(): px2 = lax.ppermute(px2, 'fine', swaps(FINE, 1))  3.02 us
    pallas_call x1, Pallas kernels, body(): pl.pallas_call(finish_kernel, in_specs=whole(12), out_specs=[pl.BlockSpec...  2.28 us
    pallas_call x1, Pallas kernels, body(): pl.pallas_call(x_faces_kernel, in_specs=[pl.BlockSpec(memory_space=pltpu....  1.46 us
  transfers between devices with their start and end apart: 4, of which 0 were waited for; matrix products, arithmetic and copies ran while one was open for 0% of the time, Pallas kernels for 15%

profile of v1, /device:TPU:9, one launch (start us, length us, event | category | flops | bytes accessed | tf_op | source)
XLA Modules:
  0.0 51.4 jit_solution(9810373528633263287)
XLA Ops:
  0.6 1.5 %x_faces.1 = (bf16[21,8,256]{2,1,0:T(8,128)(2,1)S(1)}, bf16[21,8,256]{2,1,0:T(8,128)(2,1)S(1)}, f32[12,8,8,256]{3,2,1,0:T(8,128)S(1)}, f32[9,8,8,256]{3,2,1,0:T(...) custom-call(f32[12,8,8,256]{3,2,1,0:T(8,128)} %loads_ref.1, f32[9,8,8,256]{3,2,1,0:T(8,128)} %rot_ref.1, ...), custom_call_target="tpu_custom_call" | custom-call | tf_op jit(solution)/shard_map/x_faces/pallas_call | solution.py:477
  2.1 0.0 copy-start
  2.1 0.8 %collective-permute-start = (bf16[21,8,256]{2,1,0:T(8,128)(2,1)S(1)}, bf16[21,8,256]{2,1,0:T(8,128)(2,1)S(1)}, u32[]{:S(2)}, u32[]{:S(2)}) collective-permute-start(bf16[21,8,256]{2,1,0:T(8,128)(2,1)S(1)} %get-tuple-element.27), channel_id=1, source_target_pairs={{0,4},{4,0},{8,12},{12,8},{16,20},{20,16},{24,28},{28,24},{32,36},... | collective-permute-start | bytes 258056 | tf_op jit(solution)/shard_map/ppermute | solution.py:493
  2.9 3.0 %collective-permute-start.1 = (bf16[21,8,256]{2,1,0:T(8,128)(2,1)S(1)}, bf16[21,8,256]{2,1,0:T(8,128)(2,1)S(1)}, u32[]{:S(2)}, u32[]{:S(2)}) collective-permute-start(bf16[21,8,256]{2,1,0:T(8,128)(2,1)S(1)} %get-tuple-element.28), channel_id=1, source_target_pairs={{0,0},{4,8},{8,4},{12,16},{16,12},{20,24},{24,20},{28,32},{32,28},... | collective-permute-start | bytes 258056 | tf_op jit(solution)/shard_map/ppermute | solution.py:494
  5.9 0.0 slice-start
  5.9 0.5 rows.1
  6.4 0.0 copy-start.1
  6.4 0.0 copy-start.2
  6.4 0.0 copy-start.4
  6.4 0.0 copy-start.5
  6.4 3.4 %inner_0.1.inner1_ref = f32[12,5,8,256]{3,2,1,0:T(8,128)S(1)} custom-call(f32[12,8,8,256]{3,2,1,0:T(8,128)S(1)} %get-tuple-element.19.loads_ref.low_ref.high_ref, f32[9,8,8,256]{3,2,1,0:T(8,128)S(1)} %get-tuple-element.20.rot_ref, s32[8,8,256]{2,1,0:T(8,128)S(1)} %get-tuple-element.21.occ_ref, bf16[2,192,192]{2,1,0:T(8,128)(2,1)S(1)} %get-tuple-element.24.stiff_ref), custom_call_target="tpu_custom_call" | custom-call | bytes 9600000 | tf_op jit(solution)/shard_map/inner_0/pallas_call | solution.py:506
  9.8 0.0 collective-permute-done.px1_ref
  9.8 0.0 collective-permute-done.1.px2_ref
  9.8 0.1 y_faces.1
  9.9 0.2 collective-permute-start.2
  10.2 0.0 slice-start.1
  10.2 4.2 %collective-permute-start.3 = (bf16[26,8,256]{2,1,0:T(8,128)(2,1)S(1)}, bf16[26,8,256]{2,1,0:T(8,128)(2,1)S(1)}, u32[]{:S(2)}, u32[]{:S(2)}) collective-permute-start(bf16[26,8,256]{2,1,0:T(8,128)(2,1)S(1)} %get-tuple-element.30), channel_id=1, source_target_pairs={{0,0},{1,2},{2,1},{3,3},{4,4},{5,6},{6,5},{7,7},{8,8},{9,10},{10,9... | collective-permute-start | bytes 319496 | tf_op jit(solution)/shard_map/ppermute | solution.py:533
  14.3 2.6 %inner_4.1.inner2_ref = f32[12,4,8,256]{3,2,1,0:T(8,128)S(1)} custom-call(f32[12,8,8,256]{3,2,1,0:T(8,128)S(1)} %get-tuple-element.19.loads_ref.low_ref.high_ref, f32[9,8,8,256]{3,2,1,0:T(8,128)S(1)} %get-tuple-element.20.rot_ref, s32[8,8,256]{2,1,0:T(8,128)S(1)} %get-tuple-element.21.occ_ref, bf16[2,192,192]{2,1,0:T(8,128)(2,1)S(1)} %get-tuple-element.24.stiff_ref), custom_call_target="tpu_custom_call" | custom-call | bytes 7200000 | tf_op jit(solution)/shard_map/inner_4/pallas_call | solution.py:506
  16.9 1.1 %x_edges.1.edges_ref = f32[2,12,8,256]{3,2,1,0:T(8,128)S(1)} custom-call(f32[12,8,8,256]{3,2,1,0:T(8,128)S(1)} %get-tuple-element.19.loads_ref.low_ref.high_ref, f32[12,8,8,256]{3,2,1,0:T(8,128)S(1)} %get-tuple-element.19.loads_ref.low_ref.high_ref, f32[9,8,8,256]{3,2,1,0:T(8,128)S(1)} %get-tuple-element.20.rot_ref, ...), custom_call_target="tpu_custom_call" | custom-call | bytes 4800000 | tf_op jit(solution)/shard_map/x_edges/pallas_call | solution.py:535
  18.0 0.0 copy-start.3
  18.1 0.0 collective-permute-done.2.py1_ref
  18.1 0.0 collective-permute-done.3.py2_ref
  18.1 0.0 copy-done
  18.1 2.3 %finish.1 = (f32[12,8,8,256]{3,2,1,0:T(8,128)}, bf16[256,128]{1,0:T(8,128)(2,1)S(1)}) custom-call(f32[12,8,8,256]{3,2,1,0:T(8,128)S(1)} %get-tuple-element.19.loads_ref.low_ref.high_ref, f32[12,8,256]{2,1,0:T(8,128)S(1)} %get-tuple-element.25.first_ref, f32[21,8,256]{2,1,0:T(8,128)S(1)} %get-tuple-element.26.last_ref, ...), custom_call_target="tpu_custom_call" | custom-call | tf_op jit(solution)/shard_map/finish/pallas_call | solution.py:558
  20.4 15.7 %all_to_all.10 = bf16[32,8,128]{2,1,0:T(8,128)(2,1)S(1)} all-to-all(bf16[32,8,128]{2,1,0:T(8,128)(2,1)S(1)} %bitcast.11), channel_id=1, replica_groups=mesh['fine'=32,'coarse'=4] {'fine'}, dimensions={0} | all-to-all | bytes 131072 | tf_op jit(solution)/shard_map/all_to_all | solution.py:576
  36.1 0.0 slice-done
  36.1 0.0 copy-done.1
  36.1 0.0 copy-done.2
  36.1 0.0 copy-done.4
  36.1 0.0 copy-done.5
  36.1 0.0 slice-done.1
  36.1 3.2 %lines.1 = bf16[256,128]{1,0:T(8,128)(2,1)S(1)} custom-call(bf16[256,128]{1,0:T(8,128)(2,1)S(1)} %bitcast.8, bf16[16,384,384]{2,1,0:T(8,128)(2,1)S(1)} %bitcast.7, bf16[384,32]{1,0:T(8,128)(2,1)S(1)} %copy-done.4, bf16[32,384]{1,0:T(8,128)(2,1)S(1)} %copy-done.5, bf16[2,384,128]{2,1,0:T(8,128)(2,1)S(1)} %copy-done.2, bf16[4,256,128]{2,1,0:T(8,128)(2,1)S(1)} %copy-done.1), custom_call_target="tpu_custom_call" | custom-call | tf_op jit(solution)/shard_map/lines/pallas_call | solution.py:577
  39.3 10.9 %all_to_all.11 = bf16[32,8,128]{2,1,0:T(8,128)(2,1)S(1)} all-to-all(bf16[32,8,128]{2,1,0:T(8,128)(2,1)S(1)} %bitcast.9), channel_id=1, replica_groups=mesh['fine'=32,'coarse'=4] {'fine'}, dimensions={0} | all-to-all | bytes 131072 | tf_op jit(solution)/shard_map/all_to_all | solution.py:593
  50.2 0.0 copy-done.3
  50.2 1.2 %correct.1 = f32[12,8,8,256]{3,2,1,0:T(8,128)} custom-call(f32[12,8,8,256]{3,2,1,0:T(8,128)S(1)} %get-tuple-element.19.loads_ref.low_ref.high_ref, bf16[256,128]{1,0:T(8,128)(2,1)S(1)} %bitcast.10, bf16[384,128]{1,0:T(8,128)(2,1)S(1)} %copy-done.3, bf16[2,256,256]{2,1,0:T(8,128)(2,1)S(1)} %copy-done), custom_call_target="tpu_custom_call" | custom-call | tf_op jit(solution)/shard_map/correct/pallas_call | solution.py:594
  (1 shorter events, 0.0 us)
Async XLA Ops:
  2.1 16.0 %copy-start = (bf16[2,256,256]{2,1,0:T(8,128)(2,1)S(1)}, bf16[2,256,256]{2,1,0:T(8,128)(2,1)}, u32[]{:S(2)}) copy-start(bf16[2,256,256]{2,1,0:T(8,128)(2,1)} %constant.16.clone.lift_ref) | copy-start | bytes 786436
  2.1 7.7 %collective-permute-start = (bf16[21,8,256]{2,1,0:T(8,128)(2,1)S(1)}, bf16[21,8,256]{2,1,0:T(8,128)(2,1)S(1)}, u32[]{:S(2)}, u32[]{:S(2)}) collective-permute-start(bf16[21,8,256]{2,1,0:T(8,128)(2,1)S(1)} %get-tuple-element.27), channel_id=1, source_target_pairs={{0,4},{4,0},{8,12},{12,8},{16,20},{20,16},{24,28},{28,24},{32,36},... | collective-permute-start | bytes 258056 | tf_op jit(solution)/shard_map/ppermute | solution.py:493
  2.9 6.9 %collective-permute-start.1 = (bf16[21,8,256]{2,1,0:T(8,128)(2,1)S(1)}, bf16[21,8,256]{2,1,0:T(8,128)(2,1)S(1)}, u32[]{:S(2)}, u32[]{:S(2)}) collective-permute-start(bf16[21,8,256]{2,1,0:T(8,128)(2,1)S(1)} %get-tuple-element.28), channel_id=1, source_target_pairs={{0,0},{4,8},{8,4},{12,16},{16,12},{20,24},{24,20},{28,32},{32,28},... | collective-permute-start | bytes 258056 | tf_op jit(solution)/shard_map/ppermute | solution.py:494
  5.9 30.2 %slice-start = ((s8[4718592]{0:T(1024)(128)(4,1)}), s8[4194304]{0:T(1024)(128)(4,1)S(1)}, s32[]{:S(2)}) async-start(s8[4718592]{0:T(1024)(128)(4,1)} %bitcast.5), calls=%async_computation.2 | async-start | bytes 8388608
  6.4 29.7 %copy-start.1 = (bf16[4,256,128]{2,1,0:T(8,128)(2,1)S(1)}, bf16[4,256,128]{2,1,0:T(8,128)(2,1)}, u32[]{:S(2)}) copy-start(bf16[4,256,128]{2,1,0:T(8,128)(2,1)} %constant.15.clone.fold_ref) | copy-start | bytes 786436
  6.4 29.7 %copy-start.2 = (bf16[2,384,128]{2,1,0:T(8,128)(2,1)S(1)}, bf16[2,384,128]{2,1,0:T(8,128)(2,1)}, u32[]{:S(2)}) copy-start(bf16[2,384,128]{2,1,0:T(8,128)(2,1)} %constant.14.clone.keep_ref) | copy-start | bytes 589828
  6.4 29.7 %copy-start.4 = (bf16[384,32]{1,0:T(8,128)(2,1)S(1)}, bf16[384,32]{1,0:T(8,128)(2,1)}, u32[]{:S(2)}) copy-start(bf16[384,32]{1,0:T(8,128)(2,1)} %constant.12.clone.spread_ref) | copy-start | bytes 73732
  6.4 29.7 %copy-start.5 = (bf16[32,384]{1,0:T(8,128)(2,1)S(1)}, bf16[32,384]{1,0:T(8,128)(2,1)}, u32[]{:S(2)}) copy-start(bf16[32,384]{1,0:T(8,128)(2,1)} %constant.13.clone.gather_ref) | copy-start | bytes 73732
  9.9 8.1 %collective-permute-start.2 = (bf16[26,8,256]{2,1,0:T(8,128)(2,1)S(1)}, bf16[26,8,256]{2,1,0:T(8,128)(2,1)S(1)}, u32[]{:S(2)}, u32[]{:S(2)}) collective-permute-start(bf16[26,8,256]{2,1,0:T(8,128)(2,1)S(1)} %get-tuple-element.29), channel_id=1, source_target_pairs={{0,1},{1,0},{2,3},{3,2},{4,5},{5,4},{6,7},{7,6},{8,9},{9,8},{10,11... | collective-permute-start | bytes 319496 | tf_op jit(solution)/shard_map/ppermute | solution.py:532
  10.2 25.9 %slice-start.1 = ((s8[4718592]{0:T(1024)(128)(4,1)}), s8[524288]{0:T(1024)(128)(4,1)S(1)}, s32[]{:S(2)}) async-start(s8[4718592]{0:T(1024)(128)(4,1)} %bitcast.5), calls=%async_computation.3 | async-start | bytes 1048576
  10.2 7.9 %collective-permute-start.3 = (bf16[26,8,256]{2,1,0:T(8,128)(2,1)S(1)}, bf16[26,8,256]{2,1,0:T(8,128)(2,1)S(1)}, u32[]{:S(2)}, u32[]{:S(2)}) collective-permute-start(bf16[26,8,256]{2,1,0:T(8,128)(2,1)S(1)} %get-tuple-element.30), channel_id=1, source_target_pairs={{0,0},{1,2},{2,1},{3,3},{4,4},{5,6},{6,5},{7,7},{8,8},{9,10},{10,9... | collective-permute-start | bytes 319496 | tf_op jit(solution)/shard_map/ppermute | solution.py:533
  18.0 32.1 %copy-start.3 = (bf16[384,128]{1,0:T(8,128)(2,1)S(1)}, bf16[384,128]{1,0:T(8,128)(2,1)}, u32[]{:S(2)}) copy-start(bf16[384,128]{1,0:T(8,128)(2,1)} %constant.17.clone.grown_ref) | copy-start | bytes 294916

commit v2 on v1

--- a/solution.py
+++ b/solution.py
@@ -114,7 +114,9 @@
     return low, high
 
 
-def rows_kernel(loads_ref, rot_ref, occ_ref, matrix_ref, first_ref, last_ref, stiff_ref):
+def rows_kernel(
+    loads_ref, rot_ref, occ_ref, matrix_ref, first_ref, last_ref, stiff_ref, across_ref
+):
     occ = [rooted(occ_ref[x]) for x in range(8)]
     for q in range(12):
         planes = [loads_ref[q, x] for x in range(8)]
@@ -123,17 +125,26 @@
     for k in range(9):
         planes = [rot_ref[k, x] * occ[x] for x in range(8)]
         last_ref[12 + k] = jnp.concatenate([p[7:8] for p in planes], 0)
-    tall = lax.broadcasted_iota(jnp.int32, (192, 24), 0) // 8
-    copy = (tall == lax.broadcasted_iota(jnp.int32, (192, 24), 1)).astype(bf16)
-    same = lax.broadcasted_iota(jnp.int32, (192, 192), 0) % 8
-    same = same == lax.broadcasted_iota(jnp.int32, (192, 192), 1) % 8
+    block = lax.broadcasted_iota(jnp.int32, (192, 24), 0) >> 3
+    place = (block * 11) >> 5
+    corner = (place & 3) + (place & 2) + (place >> 2) * 2
+    part = block - 3 * place
+    copy = (corner * 3 + part == lax.broadcasted_iota(jnp.int32, (192, 24), 1)).astype(bf16)
+
+    def same(size):
+        row = lax.broadcasted_iota(jnp.int32, (size, size), 0)
+        return ((row ^ lax.broadcasted_iota(jnp.int32, (size, size), 1)) & 7) == 0
+
     whole_matrix = matrix_ref[...]
     main = whole_matrix.astype(bf16)
     rest = (whole_matrix - main.astype(f32)).astype(bf16)
     for slot, part in ((0, main), (1, rest)):
         wide = jnp.dot(copy, part, preferred_element_type=f32).astype(bf16)
-        wide = lax.dot_general(wide, copy, (((1,), (1,)), ((), ())), preferred_element_type=f32)
-        stiff_ref[slot] = jnp.where(same, wide, 0.0).astype(bf16)
+        nt = (((1,), (1,)), ((), ()))
+        full = lax.dot_general(wide, copy, nt, preferred_element_type=f32)
+        stiff_ref[slot] = jnp.where(same(192), full, 0.0).astype(bf16)
+        full = lax.dot_general(wide[0:96], copy[96:192], nt, preferred_element_type=f32)
+        across_ref[slot] = jnp.where(same(96), full, 0.0).astype(bf16)
 
 
 def y_faces_kernel(first_ref, last_ref, px1_ref, px2_ref, one_ref, two_ref, near_ref, far_ref):
@@ -176,25 +187,38 @@
     ]
 
 
-def element_forces(stiff_ref, local, scale, pick):
+ORDER = (0, 1, 4, 5, 2, 3, 6, 7)
+
+
+def element_forces(main, rest, local, scale, pick, corners=ORDER):
     held, at = [], 0
-    for corner in range(8):
-        got = pick(corner)
-        held += [jnp.zeros((8, 256), f32)] * 3 if got is None else turn_in(scale, got)
+    for corner in corners:
+        held += turn_in(scale, pick(corner))
         while len(held) >= 2:
             pair = jnp.concatenate(held[:2], 0)
-            main = pair.astype(bf16)
-            local[0, 16 * at : 16 * at + 16] = main
-            local[1, 16 * at : 16 * at + 16] = (pair - main.astype(f32)).astype(bf16)
+            upper = pair.astype(bf16)
+            local[0, 16 * at : 16 * at + 16] = upper
+            local[1, 16 * at : 16 * at + 16] = (pair - upper.astype(f32)).astype(bf16)
             held, at = held[2:], at + 1
-    main, rest = stiff_ref[0], stiff_ref[1]
-    out = jnp.dot(main, local[0], preferred_element_type=f32)
-    out = out + jnp.dot(rest, local[0], preferred_element_type=f32)
-    return out + jnp.dot(main, local[1], preferred_element_type=f32)
-
-
-def corner_rows(out, corner):
-    return [out[8 * (3 * corner + j) : 8 * (3 * corner + j) + 8] for j in range(3)]
+    used = 16 * at
+    out = jnp.dot(main, local[0, 0:used], preferred_element_type=f32)
+    out = out + jnp.dot(rest, local[0, 0:used], preferred_element_type=f32)
+    return out + jnp.dot(main, local[1, 0:used], preferred_element_type=f32)
+
+
+def in_turn(steps):
+    held = None
+    for make, use in steps:
+        out = make()
+        if held is not None:
+            held[0](held[1])
+        held = (use, out)
+    held[0](held[1])
+
+
+def corner_rows(out, corner, skipped=0):
+    at = 24 * (ORDER.index(corner) - skipped)
+    return [out[at + 8 * j : at + 8 * j + 8] for j in range(3)]
 
 
 def put_nodes(nodes, p, q, v):
@@ -220,33 +244,36 @@
 
 
 def inner_kernel(start, count, loads_ref, rot_ref, occ_ref, stiff_ref, force_ref, nodes, carry, local):
-    @pl.loop(0, count + 1)
-    def _(p):
+    for p in range(count + 1):
         for q in range(12):
             put_nodes(nodes, p, q, loads_ref[q, start + p])
-
-    carry[...] = jnp.zeros_like(carry)
-
-    @pl.loop(0, count)
-    def _(e):
+    steps = []
+    for e in range(count):
         weight = rooted(occ_ref[start + e])
-        scale = [rot_ref[k, start + e] * weight for k in range(9)]
-        for case in range(4):
-            out = element_forces(stiff_ref, local.at[case], scale, picker(nodes, e, case))
+        turns = [rot_ref[k, start + e] * weight for k in range(9)]
+
+        def make(case, e=e, scale=turns):
+            pick = picker(nodes, e, case)
+            return element_forces(stiff_ref[0], stiff_ref[1], local.at[4 * e + case], scale, pick)
+
+        def use(case, out, e=e, scale=turns):
             total = [[None] * 4 for _ in range(3)]
             for corner in range(8):
                 turned = turn_out(scale, corner_rows(out, corner))
                 for i in range(3):
                     q = i * 4 + case
                     if corner % 2 == 0:
-                        total[i][corner // 2] = turned[i] + carry[corner // 2, q]
+                        past = carry[e, corner // 2, q] if e else 0.0
+                        total[i][corner // 2] = turned[i] + past
                     else:
-                        carry[corner // 2, q] = turned[i]
+                        carry[e + 1, corner // 2, q] = turned[i]
             for i in range(3):
                 force_ref[i * 4 + case, e] = settle(total[i])
 
+        steps += [(functools.partial(make, k), functools.partial(use, k)) for k in range(4)]
+    in_turn(steps)
     for q in range(12):
-        force_ref[q, count] = settle([carry[side, q] for side in range(4)])
+        force_ref[q, count] = settle([carry[count, side, q] for side in range(4)])
 
 
 def x_edges_kernel(
@@ -261,14 +288,19 @@
         low, _ = x_sides(px1_ref, px2_ref, 12 + k)
         scales[0, k] = low
         scales[1, k] = rot_ref[k, 0] * weight
-    for edge in range(2):
+    def make(edge, case):
         scale = [scales[edge, k] for k in range(9)]
-        for case in range(4):
-            at = 4 * edge + case
-            out = element_forces(stiff_ref, local.at[at], scale, picker(nodes, 2 * edge, case))
-            sides = [turn_out(scale, corner_rows(out, 2 * side + 1 - edge)) for side in range(4)]
-            for i in range(3):
-                force_ref[edge, i * 4 + case] = settle([side[i] for side in sides])
+        pick = picker(nodes, 2 * edge, case)
+        return element_forces(stiff_ref[0], stiff_ref[1], local.at[4 * edge + case], scale, pick)
+
+    def use(edge, case, out):
+        scale = [scales[edge, k] for k in range(9)]
+        sides = [turn_out(scale, corner_rows(out, 2 * side + 1 - edge)) for side in range(4)]
+        for i in range(3):
+            force_ref[edge, i * 4 + case] = settle([side[i] for side in sides])
+
+    steps = [(edge, case) for edge in range(2) for case in range(4)]
+    in_turn([(functools.partial(make, *k), functools.partial(use, *k)) for k in steps])
 
 
 def finish_kernel(
@@ -280,6 +312,7 @@
     near_ref,
     far_ref,
     stiff_ref,
+    across_ref,
     lift_ref,
     inner1_ref,
     inner2_ref,
@@ -290,10 +323,8 @@
     above,
     low,
     high,
-    made,
     local,
     sums,
-    sent,
 ):
     row = row_index()
     place = lax.axis_index("coarse")
@@ -330,20 +361,24 @@
             got.append(jnp.concatenate(rows, 0))
         return [next_z(v) for v in got] if off_z else got
 
-    out = element_forces(stiff_ref, local.at[8], scale, pick_first)
-    flat = [jnp.where(lower, u, v) for u, v in zip(corner_rows(out, 3), corner_rows(out, 1))]
-    tall = [jnp.where(lower, u, v) for u, v in zip(corner_rows(out, 7), corner_rows(out, 5))]
-    flat, tall = turn_out(scale, flat), turn_out(scale, tall)
-    ends = [flat[i] + past_z(tall[i]) for i in range(3)]
-
+    ends = []
+
+    def make_first():
+        return element_forces(stiff_ref[0], stiff_ref[1], local.at[8], scale, pick_first)
+
+    def use_first(out):
+        flat = [jnp.where(lower, u, v) for u, v in zip(corner_rows(out, 3), corner_rows(out, 1))]
+        tall = [jnp.where(lower, u, v) for u, v in zip(corner_rows(out, 7), corner_rows(out, 5))]
+        flat, tall = turn_out(scale, flat), turn_out(scale, tall)
+        ends.extend(flat[i] + past_z(tall[i]) for i in range(3))
+
+    steps = [(make_first, use_first)]
     for upper in range(2):
-        scale = [last_ref[12 + k] if upper else tile(below, 12 + k) for k in range(9)]
+        turns = [last_ref[12 + k] if upper else tile(below, 12 + k) for k in range(9)]
         for case in range(4):
 
-            def pick(corner):
+            def pick(corner, upper=upper, case=case):
                 off_x, off_y, off_z = corner % 2, corner // 2 % 2, corner // 4
-                if upper and not off_y:
-                    return None
                 got = []
                 for q in (case, 4 + case, 8 + case):
                     if not upper and off_y:
@@ -354,27 +389,36 @@
                     got.append(jnp.where(row == 7, past, pltpu.roll(v, 7, 0)) if off_x else v)
                 return [next_z(v) for v in got] if off_z else got
 
-            out = element_forces(stiff_ref, local.at[4 * upper + case], scale, pick)
-            sides = []
-            for off_x in range(2):
-                flat = turn_out(scale, corner_rows(out, off_x + 2 - 2 * upper))
-                tall = turn_out(scale, corner_rows(out, off_x + 6 - 2 * upper))
-                sides.append([flat[i] + past_z(tall[i]) for i in range(3)])
-            at = 4 * upper + case
-            for i in range(3):
-                past = jnp.where(row == 0, ends[i][at : at + 1], pltpu.roll(sides[1][i], 1, 0))
-                (low, high)[upper][i * 4 + case] = sides[0][i] + past
+            def make(upper=upper, case=case, turns=turns, pick=pick):
+                slot = local.at[4 * upper + case]
+                if upper:
+                    return element_forces(across_ref[0], across_ref[1], slot, turns, pick, ORDER[4:])
+                return element_forces(stiff_ref[0, 96:192], stiff_ref[1, 96:192], slot, turns, pick)
+
+            def use(out, upper=upper, case=case, turns=turns):
+                skipped = 0 if upper else 4
+                sides = []
+                for off_x in range(2):
+                    flat = turn_out(turns, corner_rows(out, off_x + 2 - 2 * upper, skipped))
+                    tall = turn_out(turns, corner_rows(out, off_x + 6 - 2 * upper, skipped))
+                    sides.append([flat[i] + past_z(tall[i]) for i in range(3)])
+                at = 4 * upper + case
+                for i in range(3):
+                    past = jnp.where(row == 0, ends[i][at : at + 1], pltpu.roll(sides[1][i], 1, 0))
+                    (low, high)[upper][i * 4 + case] = sides[0][i] + past
+
+            steps.append((make, use))
+    in_turn(steps)
 
     def residual_of(q, x, force):
         force = force + jnp.where(row == 0, low[q, x : x + 1], 0.0)
         force = force + jnp.where(row == 7, high[q, x : x + 1], 0.0)
         given = loads_ref[q, x]
         left = given - relax_step * (spring * given + force)
-        made[q, x] = left
+        residual_ref[q, x] = left
         return left
 
     split = inner1_ref.shape[1] - 1
-    copies = [pltpu.make_async_copy(made.at[q], residual_ref.at[q], sent.at[q]) for q in range(12)]
     for q in range(12):
         planes = []
         for x in range(8):
@@ -384,7 +428,6 @@
             if x in (0, 7):
                 force = force + edges_ref[x // 7, q]
             planes.append(residual_of(q, x, force))
-        copies[q].start()
         for half in range(2):
             s0 = planes[4 * half] + planes[4 * half + 1]
             s1 = planes[4 * half + 2] + planes[4 * half + 3]
@@ -403,13 +446,24 @@
             term = lax.dot_general(lift_ref[half], part, nt, preferred_element_type=f32)
             coarse = term if coarse is None else coarse + term
     coarse_ref[...] = coarse.astype(bf16)
-    for copy in copies:
-        copy.wait()
 
 
 def lines_kernel(
-    got_ref, inverse_ref, spread_ref, gather_ref, keep_ref, fold_ref, sent_ref, rows, back
+    got_ref,
+    inverse_ref,
+    spread_ref,
+    gather_ref,
+    keep_ref,
+    fold_ref,
+    made_ref,
+    sent_ref,
+    residual_ref,
+    rows,
+    back,
+    stored,
 ):
+    store = pltpu.make_async_copy(made_ref, residual_ref, stored)
+    store.start()
     nt = (((1,), (1,)), ((), ()))
     rows[...] = got_ref[...].astype(f32)
     vectors = jnp.zeros((384, 128), f32)
@@ -437,15 +491,16 @@
             for k in range(2):
                 back[pl.ds(2 * pair + k, 32, stride=8), :] = part[:, 128 * k : 128 * k + 128]
     sent_ref[...] = back[...].astype(bf16)
+    store.wait()
 
 
 def correct_kernel(loads_ref, back_ref, grown_ref, lift_ref, out_ref, made, sent):
     nt = (((1,), (1,)), ((), ()))
     copies = [pltpu.make_async_copy(made.at[q], out_ref.at[q], sent.at[q]) for q in range(12)]
-    tall = lax.dot_general(grown_ref[...], back_ref[...], nt, preferred_element_type=f32).astype(bf16)
     for half in range(2):
-        mine = tall[192 * half : 192 * half + 192]
-        coarse = jnp.dot(mine, lift_ref[half], preferred_element_type=f32)
+        mine = grown_ref[192 * half : 192 * half + 192]
+        mine = lax.dot_general(mine, back_ref[...], nt, preferred_element_type=f32)
+        coarse = jnp.dot(mine.astype(bf16), lift_ref[half], preferred_element_type=f32)
         for q in range(6 * half, 6 * half + 6):
             for part in range(4):
                 at = 32 * (q % 6) + 8 * part
@@ -492,11 +547,11 @@
     )(*(pltpu.with_memory_space_constraint(a, pltpu.MemorySpace.HBM) for a in (loads, rotations, occupancy, element_matrix)))
     px1 = lax.ppermute(px1, "fine", swaps(FINE, 0))
     px2 = lax.ppermute(px2, "fine", swaps(FINE, 1))
-    first, last, stiff = pl.pallas_call(
+    first, last, stiff, across = pl.pallas_call(
         rows_kernel,
         in_specs=whole(4),
-        out_specs=whole(3),
-        out_shape=(shape((12, 8, 256), f32), shape((21, 8, 256), f32), shape((2, 192, 192), bf16)),
+        out_specs=whole(4),
+        out_shape=(shape((12, 8, 256), f32), shape((21, 8, 256), f32), shape((2, 192, 192), bf16), shape((2, 96, 96), bf16)),
         compiler_params=params(8),
         cost_estimate=cost(2),
         name="rows",
@@ -510,10 +565,10 @@
             out_shape=shape((12, count + 1, 8, 256), f32),
             scratch_shapes=[
                 pltpu.VMEM((count + 1, 4, 12, 8, 256), f32),
-                pltpu.VMEM((4, 12, 8, 256), f32),
-                pltpu.VMEM((4, 2, 192, 256), bf16),
+                pltpu.VMEM((count + 1, 4, 12, 8, 256), f32),
+                pltpu.VMEM((4 * count, 2, 192, 256), bf16),
             ],
-            compiler_params=params(12),
+            compiler_params=params(20),
             cost_estimate=cost(0.8 * count),
             name=f"inner_{start}",
         )(loads, rotations, occupancy, stiff)
@@ -557,31 +612,30 @@
     )(loads, loads, rotations, occupancy, px1, px2, stiff)
     residual, coarse = pl.pallas_call(
         finish_kernel,
-        in_specs=whole(12),
-        out_specs=[pl.BlockSpec(memory_space=pltpu.MemorySpace.HBM)] + whole(1),
+        in_specs=whole(13),
+        out_specs=whole(2),
         out_shape=(shape((12, 8, 8, 256), f32), shape((256, 128), bf16)),
         scratch_shapes=[
             pltpu.VMEM((208, 256), f32),
             pltpu.VMEM((208, 256), f32),
             pltpu.VMEM((12, 8, 256), f32),
             pltpu.VMEM((12, 8, 256), f32),
-            pltpu.VMEM((12, 8, 8, 256), f32),
             pltpu.VMEM((9, 2, 192, 256), bf16),
             pltpu.VMEM((2, 128, 256), f32),
-            pltpu.SemaphoreType.DMA((12,)),
         ],
         compiler_params=params(16),
         name="finish",
-    )(loads, first, last, py1, py2, near, far, stiff, table["lift"], inner1, inner2, edges)
+    )(loads, first, last, py1, py2, near, far, stiff, across, table["lift"], inner1, inner2, edges)
     got = lax.all_to_all(coarse.reshape(32, 8, 128), "fine", 0, 0, tiled=True)
-    sent = pl.pallas_call(
+    sent, residual = pl.pallas_call(
         lines_kernel,
-        in_specs=whole(6),
-        out_specs=whole(1)[0],
-        out_shape=shape((256, 128), bf16),
+        in_specs=whole(7),
+        out_specs=whole(1) + [pl.BlockSpec(memory_space=pltpu.MemorySpace.HBM)],
+        out_shape=(shape((256, 128), bf16), shape((12, 8, 8, 256), f32)),
         scratch_shapes=[
             pltpu.VMEM((256, 128), f32),
             pltpu.VMEM((256, 128), f32),
+            pltpu.SemaphoreType.DMA,
         ],
         compiler_params=params(16),
         name="lines",
@@ -589,6 +643,7 @@
         got.reshape(256, 128),
         line_inverse.reshape(16, 384, 384),
         *(table[k] for k in ("spread", "gather", "keep", "fold")),
+        residual,
     )
     back = lax.all_to_all(sent.reshape(32, 8, 128), "fine", 0, 0, tiled=True)
     displacement = pl.pallas_call(
@@ -603,7 +658,7 @@
     return displacement, residual
 
 
-SPLIT = 4
+SPLIT = 5
 FIRST = 8 << 20
 
 def solution(mesh):

time: 51.6 us -> 49.5 us (0.959)
  Pallas kernels: 15.8 us -> 12.7 us
  blocking collectives: 26.6 us -> 27.3 us
    pallas_call x2, Pallas kernels: 5.93 us -> 3.63 us  [inner(): pl.pallas_call(functools.partial(inner_kernel, start, count), in_specs=wh...]
    all_to_all x1, blocking collectives: 15.7 us -> 16.4 us  [body(): got = lax.all_to_all(coarse.reshape(32, 8, 128), 'fine', 0, 0, tiled=True)]
    pallas_call x3, Pallas kernels: 5.91 us -> 5.21 us  [the longest x1 3.12 us: body(): pl.pallas_call(lines_kernel, in_specs=whole(7), out_specs=whole(1) + [pl....]
  transfers between devices with their start and end apart: 4 -> 4, of which waited for: 0 -> 0; matrix products, arithmetic and copies ran while one was open for 0% -> 0% of each run, Pallas kernels for 15% -> 11%
where the time goes in v2:
time: 49.5 us; the launch traced here: 49.1 us
  blocking collectives  27.3 us (55%)
  Pallas kernels  12.7 us (26%)
  starting transfers between devices  8.18 us (17%)
  between operations  0.84 us (2%)
    all_to_all x1, blocking collectives, body(): got = lax.all_to_all(coarse.reshape(32, 8, 128), 'fine', 0, 0, tiled=True)  16.4 us
    all_to_all x1, blocking collectives, body(): back = lax.all_to_all(sent.reshape(32, 8, 128), 'fine', 0, 0, tiled=True)  10.9 us
    ppermute x1, starting transfers between devices, body(): py2 = lax.ppermute(py2, 'coarse', swaps(COARSE, 1))  4.15 us
    pallas_call x2, Pallas kernels, inner(): pl.pallas_call(functools.partial(inner_kernel, start, count), in_specs=wh...  3.63 us
    pallas_call x1, Pallas kernels, body(): pl.pallas_call(lines_kernel, in_specs=whole(7), out_specs=whole(1) + [pl....  3.12 us
    ppermute x1, starting transfers between devices, body(): px2 = lax.ppermute(px2, 'fine', swaps(FINE, 1))  3.02 us
    pallas_call x1, Pallas kernels, body(): pl.pallas_call(finish_kernel, in_specs=whole(13), out_specs=whole(2), out...  1.47 us
    pallas_call x1, Pallas kernels, body(): pl.pallas_call(x_faces_kernel, in_specs=[pl.BlockSpec(memory_space=pltpu....  1.46 us
  transfers between devices with their start and end apart: 4, of which 0 were waited for; matrix products, arithmetic and copies ran while one was open for 0% of the time, Pallas kernels for 11%

profile of v2, /device:TPU:9, one launch (start us, length us, event | category | flops | bytes accessed | tf_op | source)
XLA Modules:
  0.0 49.1 jit_solution(11266035899498529763)
XLA Ops:
  0.6 1.5 %x_faces.1 = (bf16[21,8,256]{2,1,0:T(8,128)(2,1)S(1)}, bf16[21,8,256]{2,1,0:T(8,128)(2,1)S(1)}, f32[12,8,8,256]{3,2,1,0:T(8,128)S(1)}, f32[9,8,8,256]{3,2,1,0:T(...) custom-call(f32[12,8,8,256]{3,2,1,0:T(8,128)} %loads_ref.1, f32[9,8,8,256]{3,2,1,0:T(8,128)} %rot_ref.1, ...), custom_call_target="tpu_custom_call" | custom-call | tf_op jit(solution)/shard_map/x_faces/pallas_call | solution.py:532
  2.1 0.0 copy-start
  2.1 0.8 %collective-permute-start = (bf16[21,8,256]{2,1,0:T(8,128)(2,1)S(1)}, bf16[21,8,256]{2,1,0:T(8,128)(2,1)S(1)}, u32[]{:S(2)}, u32[]{:S(2)}) collective-permute-start(bf16[21,8,256]{2,1,0:T(8,128)(2,1)S(1)} %get-tuple-element.30), channel_id=1, source_target_pairs={{0,4},{4,0},{8,12},{12,8},{16,20},{20,16},{24,28},{28,24},{32,36},... | collective-permute-start | bytes 258056 | tf_op jit(solution)/shard_map/ppermute | solution.py:548
  2.9 3.0 %collective-permute-start.1 = (bf16[21,8,256]{2,1,0:T(8,128)(2,1)S(1)}, bf16[21,8,256]{2,1,0:T(8,128)(2,1)S(1)}, u32[]{:S(2)}, u32[]{:S(2)}) collective-permute-start(bf16[21,8,256]{2,1,0:T(8,128)(2,1)S(1)} %get-tuple-element.31), channel_id=1, source_target_pairs={{0,0},{4,8},{8,4},{12,16},{16,12},{20,24},{24,20},{28,32},{32,28},... | collective-permute-start | bytes 258056 | tf_op jit(solution)/shard_map/ppermute | solution.py:549
  5.9 0.0 slice-start
  5.9 0.6 %rows.1 = (f32[12,8,256]{2,1,0:T(8,128)S(1)}, f32[21,8,256]{2,1,0:T(8,128)S(1)}, bf16[2,192,192]{2,1,0:T(8,128)(2,1)S(1)}, bf16[2,96,96]{2,1,0:T(8,128)(2,1)S(1)}) custom-call(f32[12,8,8,256]{3,2,1,0:T(8,128)S(1)} %get-tuple-element.22.loads_ref.low_ref.high_ref, f32[9,8,8,256]{3,2,1,0:T(8,128)S(1)} %get-tuple-element.23.rot_ref, ...), custom_call_target="tpu_custom_call" | custom-call | bytes 6000000 | tf_op jit(solution)/shard_map/rows/pallas_call | solution.py:550
  6.5 0.0 copy-start.1
  6.5 0.0 copy-start.2
  6.5 0.0 copy-start.4
  6.6 0.0 copy-start.5
  6.6 2.5 %inner_0.1.inner1_ref = f32[12,6,8,256]{3,2,1,0:T(8,128)S(1)} custom-call(f32[12,8,8,256]{3,2,1,0:T(8,128)S(1)} %get-tuple-element.22.loads_ref.low_ref.high_ref, f32[9,8,8,256]{3,2,1,0:T(8,128)S(1)} %get-tuple-element.23.rot_ref, s32[8,8,256]{2,1,0:T(8,128)S(1)} %get-tuple-element.24.occ_ref, bf16[2,192,192]{2,1,0:T(8,128)(2,1)S(1)} %get-tuple-element.27.stiff_ref), custom_call_target="tpu_custom_call" | custom-call | bytes 12000000 | tf_op jit(solution)/shard_map/inner_0/pallas_call | solution.py:561
  9.1 0.0 collective-permute-done.px1_ref
  9.1 0.0 collective-permute-done.1.px2_ref
  9.1 0.1 y_faces.1
  9.2 0.3 collective-permute-start.2
  9.5 0.0 slice-start.1
  9.5 4.2 %collective-permute-start.3 = (bf16[26,8,256]{2,1,0:T(8,128)(2,1)S(1)}, bf16[26,8,256]{2,1,0:T(8,128)(2,1)S(1)}, u32[]{:S(2)}, u32[]{:S(2)}) collective-permute-start(bf16[26,8,256]{2,1,0:T(8,128)(2,1)S(1)} %get-tuple-element.33), channel_id=1, source_target_pairs={{0,0},{1,2},{2,1},{3,3},{4,4},{5,6},{6,5},{7,7},{8,8},{9,10},{10,9... | collective-permute-start | bytes 319496 | tf_op jit(solution)/shard_map/ppermute | solution.py:588
  13.7 1.1 %inner_5.1.inner2_ref = f32[12,3,8,256]{3,2,1,0:T(8,128)S(1)} custom-call(f32[12,8,8,256]{3,2,1,0:T(8,128)S(1)} %get-tuple-element.22.loads_ref.low_ref.high_ref, f32[9,8,8,256]{3,2,1,0:T(8,128)S(1)} %get-tuple-element.23.rot_ref, s32[8,8,256]{2,1,0:T(8,128)S(1)} %get-tuple-element.24.occ_ref, bf16[2,192,192]{2,1,0:T(8,128)(2,1)S(1)} %get-tuple-element.27.stiff_ref), custom_call_target="tpu_custom_call" | custom-call | bytes 4800000 | tf_op jit(solution)/shard_map/inner_5/pallas_call | solution.py:561
  14.8 1.1 %x_edges.1.edges_ref = f32[2,12,8,256]{3,2,1,0:T(8,128)S(1)} custom-call(f32[12,8,8,256]{3,2,1,0:T(8,128)S(1)} %get-tuple-element.22.loads_ref.low_ref.high_ref, f32[12,8,8,256]{3,2,1,0:T(8,128)S(1)} %get-tuple-element.22.loads_ref.low_ref.high_ref, f32[9,8,8,256]{3,2,1,0:T(8,128)S(1)} %get-tuple-element.23.rot_ref, ...), custom_call_target="tpu_custom_call" | custom-call | bytes 4800000 | tf_op jit(solution)/shard_map/x_edges/pallas_call | solution.py:590
  15.9 0.0 copy-start.3
  15.9 0.0 collective-permute-done.2.py1_ref
  15.9 0.0 collective-permute-done.3.py2_ref
  15.9 0.0 copy-done
  15.9 1.5 %finish.1 = (f32[12,8,8,256]{3,2,1,0:T(8,128)S(1)}, bf16[256,128]{1,0:T(8,128)(2,1)S(1)}) custom-call(f32[12,8,8,256]{3,2,1,0:T(8,128)S(1)} %get-tuple-element.22.loads_ref.low_ref.high_ref, f32[12,8,256]{2,1,0:T(8,128)S(1)} %get-tuple-element.28.first_ref, f32[21,8,256]{2,1,0:T(8,128)S(1)} %get-tuple-element.29.last_ref, ...), custom_call_target="tpu_custom_call" | custom-call | tf_op jit(solution)/shard_map/finish/pallas_call | solution.py:613
  17.4 16.4 %all_to_all.10 = bf16[32,8,128]{2,1,0:T(8,128)(2,1)S(1)} all-to-all(bf16[32,8,128]{2,1,0:T(8,128)(2,1)S(1)} %bitcast.10), channel_id=1, replica_groups=mesh['fine'=32,'coarse'=4] {'fine'}, dimensions={0} | all-to-all | bytes 131072 | tf_op jit(solution)/shard_map/all_to_all | solution.py:629
  33.8 0.0 slice-done
  33.8 0.0 copy-done.1
  33.8 0.0 copy-done.2
  33.8 0.0 copy-done.4
  33.8 0.0 copy-done.5
  33.8 0.0 slice-done.1
  33.9 3.1 %lines.1 = (bf16[256,128]{1,0:T(8,128)(2,1)S(1)}, f32[12,8,8,256]{3,2,1,0:T(8,128)}) custom-call(bf16[256,128]{1,0:T(8,128)(2,1)S(1)} %bitcast.8, bf16[16,384,384]{2,1,0:T(8,128)(2,1)S(1)} %bitcast.7, bf16[384,32]{1,0:T(8,128)(2,1)S(1)} %copy-done.4, bf16[32,384]{1,0:T(8,128)(2,1)S(1)} %copy-done.5, bf16[2,384,128]{2,1,0:T(8,128)(2,1)S(1)} %copy-done.2, ...), custom_call_target="tpu_custom_call" | custom-call | tf_op jit(solution)/shard_map/lines/pallas_call | solution.py:630
  37.0 10.9 %all_to_all.11 = bf16[32,8,128]{2,1,0:T(8,128)(2,1)S(1)} all-to-all(bf16[32,8,128]{2,1,0:T(8,128)(2,1)S(1)} %bitcast.11), channel_id=1, replica_groups=mesh['fine'=32,'coarse'=4] {'fine'}, dimensions={0} | all-to-all | bytes 131072 | tf_op jit(solution)/shard_map/all_to_all | solution.py:648
  47.9 0.0 copy-done.3
  47.9 1.2 %correct.1 = f32[12,8,8,256]{3,2,1,0:T(8,128)} custom-call(f32[12,8,8,256]{3,2,1,0:T(8,128)S(1)} %get-tuple-element.22.loads_ref.low_ref.high_ref, bf16[256,128]{1,0:T(8,128)(2,1)S(1)} %bitcast.9, bf16[384,128]{1,0:T(8,128)(2,1)S(1)} %copy-done.3, bf16[2,256,256]{2,1,0:T(8,128)(2,1)S(1)} %copy-done), custom_call_target="tpu_custom_call" | custom-call | tf_op jit(solution)/shard_map/correct/pallas_call | solution.py:649
  (1 shorter events, 0.0 us)
Async XLA Ops:
  2.1 13.8 %copy-start = (bf16[2,256,256]{2,1,0:T(8,128)(2,1)S(1)}, bf16[2,256,256]{2,1,0:T(8,128)(2,1)}, u32[]{:S(2)}) copy-start(bf16[2,256,256]{2,1,0:T(8,128)(2,1)} %constant.16.clone.lift_ref) | copy-start | bytes 786436
  2.1 7.0 %collective-permute-start = (bf16[21,8,256]{2,1,0:T(8,128)(2,1)S(1)}, bf16[21,8,256]{2,1,0:T(8,128)(2,1)S(1)}, u32[]{:S(2)}, u32[]{:S(2)}) collective-permute-start(bf16[21,8,256]{2,1,0:T(8,128)(2,1)S(1)} %get-tuple-element.30), channel_id=1, source_target_pairs={{0,4},{4,0},{8,12},{12,8},{16,20},{20,16},{24,28},{28,24},{32,36},... | collective-permute-start | bytes 258056 | tf_op jit(solution)/shard_map/ppermute | solution.py:548
  2.9 6.3 %collective-permute-start.1 = (bf16[21,8,256]{2,1,0:T(8,128)(2,1)S(1)}, bf16[21,8,256]{2,1,0:T(8,128)(2,1)S(1)}, u32[]{:S(2)}, u32[]{:S(2)}) collective-permute-start(bf16[21,8,256]{2,1,0:T(8,128)(2,1)S(1)} %get-tuple-element.31), channel_id=1, source_target_pairs={{0,0},{4,8},{8,4},{12,16},{16,12},{20,24},{24,20},{28,32},{32,28},... | collective-permute-start | bytes 258056 | tf_op jit(solution)/shard_map/ppermute | solution.py:549
  5.9 27.9 %slice-start = ((s8[4718592]{0:T(1024)(128)(4,1)}), s8[4194304]{0:T(1024)(128)(4,1)S(1)}, s32[]{:S(2)}) async-start(s8[4718592]{0:T(1024)(128)(4,1)} %bitcast.5), calls=%async_computation.2 | async-start | bytes 8388608
  6.5 27.3 %copy-start.1 = (bf16[4,256,128]{2,1,0:T(8,128)(2,1)S(1)}, bf16[4,256,128]{2,1,0:T(8,128)(2,1)}, u32[]{:S(2)}) copy-start(bf16[4,256,128]{2,1,0:T(8,128)(2,1)} %constant.15.clone.fold_ref) | copy-start | bytes 786436
  6.5 27.3 %copy-start.2 = (bf16[2,384,128]{2,1,0:T(8,128)(2,1)S(1)}, bf16[2,384,128]{2,1,0:T(8,128)(2,1)}, u32[]{:S(2)}) copy-start(bf16[2,384,128]{2,1,0:T(8,128)(2,1)} %constant.14.clone.keep_ref) | copy-start | bytes 589828
  6.5 27.3 %copy-start.4 = (bf16[384,32]{1,0:T(8,128)(2,1)S(1)}, bf16[384,32]{1,0:T(8,128)(2,1)}, u32[]{:S(2)}) copy-start(bf16[384,32]{1,0:T(8,128)(2,1)} %constant.12.clone.spread_ref) | copy-start | bytes 73732
  6.6 27.3 %copy-start.5 = (bf16[32,384]{1,0:T(8,128)(2,1)S(1)}, bf16[32,384]{1,0:T(8,128)(2,1)}, u32[]{:S(2)}) copy-start(bf16[32,384]{1,0:T(8,128)(2,1)} %constant.13.clone.gather_ref) | copy-start | bytes 73732
  9.2 6.6 %collective-permute-start.2 = (bf16[26,8,256]{2,1,0:T(8,128)(2,1)S(1)}, bf16[26,8,256]{2,1,0:T(8,128)(2,1)S(1)}, u32[]{:S(2)}, u32[]{:S(2)}) collective-permute-start(bf16[26,8,256]{2,1,0:T(8,128)(2,1)S(1)} %get-tuple-element.32), channel_id=1, source_target_pairs={{0,1},{1,0},{2,3},{3,2},{4,5},{5,4},{6,7},{7,6},{8,9},{9,8},{10,11... | collective-permute-start | bytes 319496 | tf_op jit(solution)/shard_map/ppermute | solution.py:587
  9.5 24.3 %slice-start.1 = ((s8[4718592]{0:T(1024)(128)(4,1)}), s8[524288]{0:T(1024)(128)(4,1)S(1)}, s32[]{:S(2)}) async-start(s8[4718592]{0:T(1024)(128)(4,1)} %bitcast.5), calls=%async_computation.3 | async-start | bytes 1048576
  9.5 6.4 %collective-permute-start.3 = (bf16[26,8,256]{2,1,0:T(8,128)(2,1)S(1)}, bf16[26,8,256]{2,1,0:T(8,128)(2,1)S(1)}, u32[]{:S(2)}, u32[]{:S(2)}) collective-permute-start(bf16[26,8,256]{2,1,0:T(8,128)(2,1)S(1)} %get-tuple-element.33), channel_id=1, source_target_pairs={{0,0},{1,2},{2,1},{3,3},{4,4},{5,6},{6,5},{7,7},{8,8},{9,10},{10,9... | collective-permute-start | bytes 319496 | tf_op jit(solution)/shard_map/ppermute | solution.py:588
  15.9 32.0 %copy-start.3 = (bf16[384,128]{1,0:T(8,128)(2,1)S(1)}, bf16[384,128]{1,0:T(8,128)(2,1)}, u32[]{:S(2)}) copy-start(bf16[384,128]{1,0:T(8,128)(2,1)} %constant.17.clone.grown_ref) | copy-start | bytes 294916

commit v3 on v2

--- a/solution.py
+++ b/solution.py
@@ -74,35 +74,29 @@
 
 
 def x_faces_kernel(
-    loads_ref, rot_ref, occ_ref, matrix_ref, one_ref, two_ref, loads_out, rot_out, occ_out, matrix_out, arrived
+    loads_ref, rot_ref, occ_ref, matrix_ref, one_ref, two_ref, matrix_out, faces, turns, bone, arrived
 ):
-    face = [
-        pltpu.make_async_copy(loads_ref.at[:, 0], loads_out.at[:, 0], arrived.at[0]),
-        pltpu.make_async_copy(loads_ref.at[:, 7], loads_out.at[:, 7], arrived.at[1]),
-        pltpu.make_async_copy(rot_ref.at[:, 7], rot_out.at[:, 7], arrived.at[2]),
-        pltpu.make_async_copy(occ_ref, occ_out, arrived.at[3]),
+    copies = [
+        pltpu.make_async_copy(loads_ref.at[:, 0], faces.at[0], arrived.at[0]),
+        pltpu.make_async_copy(loads_ref.at[:, 7], faces.at[1], arrived.at[1]),
+        pltpu.make_async_copy(rot_ref.at[:, 7], turns, arrived.at[2]),
+        pltpu.make_async_copy(occ_ref.at[7], bone, arrived.at[3]),
+        pltpu.make_async_copy(matrix_ref, matrix_out, arrived.at[4]),
     ]
-    rest = [
-        pltpu.make_async_copy(loads_ref.at[:, 1:7], loads_out.at[:, 1:7], arrived.at[4]),
-        pltpu.make_async_copy(rot_ref.at[:, 0:7], rot_out.at[:, 0:7], arrived.at[5]),
-        pltpu.make_async_copy(matrix_ref, matrix_out, arrived.at[6]),
-    ]
-    for copy in face + rest:
+    for copy in copies:
         copy.start()
     even = lax.axis_index("fine") % 2 == 0
-    for copy in face:
+    for copy in copies:
         copy.wait()
-    weight = rooted(occ_out[7])
+    weight = rooted(bone[...])
     for q in range(12):
-        low, high = loads_out[q, 0], loads_out[q, 7]
+        low, high = faces[0, q], faces[1, q]
         one_ref[q] = jnp.where(even, high, low).astype(bf16)
         two_ref[q] = jnp.where(even, low, high).astype(bf16)
     for k in range(9):
-        scaled = (rot_out[k, 7] * weight).astype(bf16)
+        scaled = (turns[k] * weight).astype(bf16)
         one_ref[12 + k] = scaled
         two_ref[12 + k] = scaled
-    for copy in rest:
-        copy.wait()
 
 
 def x_sides(one_ref, two_ref, k):
@@ -115,16 +109,26 @@
 
 
 def rows_kernel(
-    loads_ref, rot_ref, occ_ref, matrix_ref, first_ref, last_ref, stiff_ref, across_ref
+    loads_hbm,
+    rot_hbm,
+    occ_hbm,
+    matrix_ref,
+    loads_ref,
+    rot_ref,
+    occ_ref,
+    first_ref,
+    last_ref,
+    stiff_ref,
+    across_ref,
+    arrived,
 ):
-    occ = [rooted(occ_ref[x]) for x in range(8)]
-    for q in range(12):
-        planes = [loads_ref[q, x] for x in range(8)]
-        first_ref[q] = jnp.concatenate([p[0:1] for p in planes], 0)
-        last_ref[q] = jnp.concatenate([p[7:8] for p in planes], 0)
-    for k in range(9):
-        planes = [rot_ref[k, x] * occ[x] for x in range(8)]
-        last_ref[12 + k] = jnp.concatenate([p[7:8] for p in planes], 0)
+    copies = [
+        pltpu.make_async_copy(loads_hbm, loads_ref, arrived.at[0]),
+        pltpu.make_async_copy(rot_hbm, rot_ref, arrived.at[1]),
+        pltpu.make_async_copy(occ_hbm, occ_ref, arrived.at[2]),
+    ]
+    for copy in copies:
+        copy.start()
     block = lax.broadcasted_iota(jnp.int32, (192, 24), 0) >> 3
     place = (block * 11) >> 5
     corner = (place & 3) + (place & 2) + (place >> 2) * 2
@@ -145,6 +149,16 @@
         stiff_ref[slot] = jnp.where(same(192), full, 0.0).astype(bf16)
         full = lax.dot_general(wide[0:96], copy[96:192], nt, preferred_element_type=f32)
         across_ref[slot] = jnp.where(same(96), full, 0.0).astype(bf16)
+    for copy in copies:
+        copy.wait()
+    occ = [rooted(occ_ref[x]) for x in range(8)]
+    for q in range(12):
+        planes = [loads_ref[q, x] for x in range(8)]
+        first_ref[q] = jnp.concatenate([p[0:1] for p in planes], 0)
+        last_ref[q] = jnp.concatenate([p[7:8] for p in planes], 0)
+    for k in range(9):
+        planes = [rot_ref[k, x] * occ[x] for x in range(8)]
+        last_ref[12 + k] = jnp.concatenate([p[7:8] for p in planes], 0)
 
 
 def y_faces_kernel(first_ref, last_ref, px1_ref, px2_ref, one_ref, two_ref, near_ref, far_ref):
@@ -529,33 +543,45 @@
     shape = jax.ShapeDtypeStruct
     face = shape((21, 8, 256), bf16)
     plane = lambda count, at: pl.BlockSpec((count, 1, 8, 256), lambda i: (0, at, 0, 0))
-    px1, px2, loads, rotations, occupancy, matrix = pl.pallas_call(
+    held = [
+        pltpu.with_memory_space_constraint(a, pltpu.MemorySpace.HBM)
+        for a in (loads, rotations, occupancy, element_matrix)
+    ]
+    in_hbm = pl.BlockSpec(memory_space=pltpu.MemorySpace.HBM)
+    px1, px2, matrix = pl.pallas_call(
         x_faces_kernel,
-        in_specs=[pl.BlockSpec(memory_space=pltpu.MemorySpace.HBM)] * 4,
-        out_specs=whole(6),
+        in_specs=[in_hbm] * 4,
+        out_specs=whole(3),
+        out_shape=(face, face, shape((24, 24), f32)),
+        scratch_shapes=[
+            pltpu.VMEM((2, 12, 8, 256), f32),
+            pltpu.VMEM((9, 8, 256), f32),
+            pltpu.VMEM((8, 256), jnp.int32),
+            pltpu.SemaphoreType.DMA((5,)),
+        ],
+        compiler_params=params(8),
+        name="x_faces",
+    )(*held)
+    px1 = lax.ppermute(px1, "fine", swaps(FINE, 0))
+    px2 = lax.ppermute(px2, "fine", swaps(FINE, 1))
+    loads, rotations, occupancy, first, last, stiff, across = pl.pallas_call(
+        rows_kernel,
+        in_specs=[in_hbm] * 3 + whole(1),
+        out_specs=whole(7),
         out_shape=(
-            face,
-            face,
             shape(loads.shape, f32),
             shape(rotations.shape, f32),
             shape(occupancy.shape, jnp.int32),
-            shape((24, 24), f32),
+            shape((12, 8, 256), f32),
+            shape((21, 8, 256), f32),
+            shape((2, 192, 192), bf16),
+            shape((2, 96, 96), bf16),
         ),
-        scratch_shapes=[pltpu.SemaphoreType.DMA((7,))],
-        compiler_params=pltpu.CompilerParams(vmem_limit_bytes=FIRST),
-        name="x_faces",
-    )(*(pltpu.with_memory_space_constraint(a, pltpu.MemorySpace.HBM) for a in (loads, rotations, occupancy, element_matrix)))
-    px1 = lax.ppermute(px1, "fine", swaps(FINE, 0))
-    px2 = lax.ppermute(px2, "fine", swaps(FINE, 1))
-    first, last, stiff, across = pl.pallas_call(
-        rows_kernel,
-        in_specs=whole(4),
-        out_specs=whole(4),
-        out_shape=(shape((12, 8, 256), f32), shape((21, 8, 256), f32), shape((2, 192, 192), bf16), shape((2, 96, 96), bf16)),
+        scratch_shapes=[pltpu.SemaphoreType.DMA((3,))],
         compiler_params=params(8),
         cost_estimate=cost(2),
         name="rows",
-    )(loads, rotations, occupancy, matrix)
+    )(*held[:3], matrix)
 
     def inner(start, count):
         return pl.pallas_call(
@@ -658,8 +684,7 @@
     return displacement, residual
 
 
-SPLIT = 5
-FIRST = 8 << 20
+SPLIT = 3
 
 def solution(mesh):
     in_specs = (

time: 49.5 us -> 49.9 us (level)
  Pallas kernels: 12.7 us -> 13.4 us
    pallas_call x2, Pallas kernels: 2.07 us -> 2.71 us  [the longest x1 1.65 us: body(): pl.pallas_call(rows_kernel, in_specs=[in_hbm] * 3 + whole(1), out_specs=w...]
  transfers between devices with their start and end apart: 4 -> 4, of which waited for: 0 -> 0; matrix products, arithmetic and copies ran while one was open for 0% -> 0% of each run, Pallas kernels for 11% -> 13%
where the time goes in v3:
time: 49.9 us; the launch traced here: 49.6 us
  blocking collectives  27.1 us (54%)
  Pallas kernels  13.4 us (27%)
  starting transfers between devices  8.18 us (16%)
  between operations  0.84 us (2%)
    all_to_all x1, blocking collectives, body(): got = lax.all_to_all(coarse.reshape(32, 8, 128), 'fine', 0, 0, tiled=True)  16.2 us
    all_to_all x1, blocking collectives, body(): back = lax.all_to_all(sent.reshape(32, 8, 128), 'fine', 0, 0, tiled=True)  10.9 us
    ppermute x1, starting transfers between devices, body(): py2 = lax.ppermute(py2, 'coarse', swaps(COARSE, 1))  4.16 us
    pallas_call x2, Pallas kernels, inner(): pl.pallas_call(functools.partial(inner_kernel, start, count), in_specs=wh...  3.68 us
    pallas_call x1, Pallas kernels, body(): pl.pallas_call(lines_kernel, in_specs=whole(7), out_specs=whole(1) + [pl....  3.12 us
    ppermute x1, starting transfers between devices, body(): px2 = lax.ppermute(px2, 'fine', swaps(FINE, 1))  3.02 us
    pallas_call x1, Pallas kernels, body(): pl.pallas_call(rows_kernel, in_specs=[in_hbm] * 3 + whole(1), out_specs=w...  1.65 us
    pallas_call x1, Pallas kernels, body(): pl.pallas_call(finish_kernel, in_specs=whole(13), out_specs=whole(2), out...  1.47 us
  transfers between devices with their start and end apart: 4, of which 0 were waited for; matrix products, arithmetic and copies ran while one was open for 0% of the time, Pallas kernels for 13%

profile of v3, /device:TPU:9, one launch (start us, length us, event | category | flops | bytes accessed | tf_op | source)
XLA Modules:
  0.0 49.6 jit_solution(13839257945633496690)
XLA Ops:
  0.6 1.1 %x_faces.1 = (bf16[21,8,256]{2,1,0:T(8,128)(2,1)S(1)}, bf16[21,8,256]{2,1,0:T(8,128)(2,1)S(1)}, f32[24,24]{1,0:T(8,128)S(1)}) custom-call(f32[12,8,8,256]{3,2,1,0:T(8,128)} %loads_hbm.1, f32[9,8,8,256]{3,2,1,0:T(8,128)} %rot_hbm.1, s32[8,8,256]{2,1,0:T(8,128)} %occ_hbm.1, f32[24,24]{1,0:T(8,128)} %matrix_ref.1), custom_call_target="tpu_custom_call" | custom-call | tf_op jit(solution)/shard_map/x_faces/pallas_call | solution.py:551
  1.7 0.0 copy-start
  1.7 0.8 %collective-permute-start = (bf16[21,8,256]{2,1,0:T(8,128)(2,1)S(1)}, bf16[21,8,256]{2,1,0:T(8,128)(2,1)S(1)}, u32[]{:S(2)}, u32[]{:S(2)}) collective-permute-start(bf16[21,8,256]{2,1,0:T(8,128)(2,1)S(1)} %get-tuple-element.30), channel_id=1, source_target_pairs={{0,4},{4,0},{8,12},{12,8},{16,20},{20,16},{24,28},{28,24},{32,36},... | collective-permute-start | bytes 258056 | tf_op jit(solution)/shard_map/ppermute | solution.py:565
  2.5 3.0 %collective-permute-start.1 = (bf16[21,8,256]{2,1,0:T(8,128)(2,1)S(1)}, bf16[21,8,256]{2,1,0:T(8,128)(2,1)S(1)}, u32[]{:S(2)}, u32[]{:S(2)}) collective-permute-start(bf16[21,8,256]{2,1,0:T(8,128)(2,1)S(1)} %get-tuple-element.31), channel_id=1, source_target_pairs={{0,0},{4,8},{8,4},{12,16},{16,12},{20,24},{24,20},{28,32},{32,28},... | collective-permute-start | bytes 258056 | tf_op jit(solution)/shard_map/ppermute | solution.py:566
  5.5 0.0 slice-start
  5.5 1.6 %rows.1 = (f32[12,8,8,256]{3,2,1,0:T(8,128)S(1)}, f32[9,8,8,256]{3,2,1,0:T(8,128)S(1)}, s32[8,8,256]{2,1,0:T(8,128)S(1)}, f32[12,8,256]{2,1,0:T(8,128)S(1)}, f32...) custom-call(f32[12,8,8,256]{3,2,1,0:T(8,128)} %loads_hbm.1, ...), custom_call_target="tpu_custom_call" | custom-call | bytes 6000000 | tf_op jit(solution)/shard_map/rows/pallas_call | solution.py:567
  7.2 1.6 %inner_0.1.inner1_ref = f32[12,4,8,256]{3,2,1,0:T(8,128)S(1)} custom-call(f32[12,8,8,256]{3,2,1,0:T(8,128)S(1)} %get-tuple-element.23.loads_ref.low_ref.high_ref, f32[9,8,8,256]{3,2,1,0:T(8,128)S(1)} %get-tuple-element.25.rot_ref, s32[8,8,256]{2,1,0:T(8,128)S(1)} %get-tuple-element.26.occ_ref, bf16[2,192,192]{2,1,0:T(8,128)(2,1)S(1)} %get-tuple-element.27.stiff_ref), custom_call_target="tpu_custom_call" | custom-call | bytes 7200000 | tf_op jit(solution)/shard_map/inner_0/pallas_call | solution.py:587
  8.8 0.0 copy-start.1
  8.8 0.0 copy-start.2
  8.8 0.0 copy-start.4
  8.8 0.0 copy-start.5
  8.8 0.0 collective-permute-done.px1_ref
  8.8 0.0 collective-permute-done.1.px2_ref
  8.8 0.1 y_faces.1
  8.9 0.2 collective-permute-start.2
  9.2 0.0 slice-start.1
  9.2 4.2 %collective-permute-start.3 = (bf16[26,8,256]{2,1,0:T(8,128)(2,1)S(1)}, bf16[26,8,256]{2,1,0:T(8,128)(2,1)S(1)}, u32[]{:S(2)}, u32[]{:S(2)}) collective-permute-start(bf16[26,8,256]{2,1,0:T(8,128)(2,1)S(1)} %get-tuple-element.33), channel_id=1, source_target_pairs={{0,0},{1,2},{2,1},{3,3},{4,4},{5,6},{6,5},{7,7},{8,8},{9,10},{10,9... | collective-permute-start | bytes 319496 | tf_op jit(solution)/shard_map/ppermute | solution.py:614
  13.4 2.1 %inner_3.1.inner2_ref = f32[12,5,8,256]{3,2,1,0:T(8,128)S(1)} custom-call(f32[12,8,8,256]{3,2,1,0:T(8,128)S(1)} %get-tuple-element.23.loads_ref.low_ref.high_ref, f32[9,8,8,256]{3,2,1,0:T(8,128)S(1)} %get-tuple-element.25.rot_ref, s32[8,8,256]{2,1,0:T(8,128)S(1)} %get-tuple-element.26.occ_ref, bf16[2,192,192]{2,1,0:T(8,128)(2,1)S(1)} %get-tuple-element.27.stiff_ref), custom_call_target="tpu_custom_call" | custom-call | bytes 9600000 | tf_op jit(solution)/shard_map/inner_3/pallas_call | solution.py:587
  15.5 1.1 %x_edges.1.edges_ref = f32[2,12,8,256]{3,2,1,0:T(8,128)S(1)} custom-call(f32[12,8,8,256]{3,2,1,0:T(8,128)S(1)} %get-tuple-element.23.loads_ref.low_ref.high_ref, f32[12,8,8,256]{3,2,1,0:T(8,128)S(1)} %get-tuple-element.23.loads_ref.low_ref.high_ref, f32[9,8,8,256]{3,2,1,0:T(8,128)S(1)} %get-tuple-element.25.rot_ref, ...), custom_call_target="tpu_custom_call" | custom-call | bytes 4800000 | tf_op jit(solution)/shard_map/x_edges/pallas_call | solution.py:616
  16.6 0.0 copy-start.3
  16.6 0.0 collective-permute-done.2.py1_ref
  16.6 0.0 collective-permute-done.3.py2_ref
  16.6 0.0 copy-done
  16.6 1.5 %finish.1 = (f32[12,8,8,256]{3,2,1,0:T(8,128)S(1)}, bf16[256,128]{1,0:T(8,128)(2,1)S(1)}) custom-call(f32[12,8,8,256]{3,2,1,0:T(8,128)S(1)} %get-tuple-element.23.loads_ref.low_ref.high_ref, f32[12,8,256]{2,1,0:T(8,128)S(1)} %get-tuple-element.28.first_ref, f32[21,8,256]{2,1,0:T(8,128)S(1)} %get-tuple-element.29.last_ref, ...), custom_call_target="tpu_custom_call" | custom-call | tf_op jit(solution)/shard_map/finish/pallas_call | solution.py:639
  18.1 16.2 %all_to_all.10 = bf16[32,8,128]{2,1,0:T(8,128)(2,1)S(1)} all-to-all(bf16[32,8,128]{2,1,0:T(8,128)(2,1)S(1)} %bitcast.10), channel_id=1, replica_groups=mesh['fine'=32,'coarse'=4] {'fine'}, dimensions={0} | all-to-all | bytes 131072 | tf_op jit(solution)/shard_map/all_to_all | solution.py:655
  34.3 0.0 slice-done
  34.3 0.0 copy-done.1
  34.3 0.0 copy-done.2
  34.4 0.0 copy-done.4
  34.4 0.0 copy-done.5
  34.4 0.0 slice-done.1
  34.4 3.1 %lines.1 = (bf16[256,128]{1,0:T(8,128)(2,1)S(1)}, f32[12,8,8,256]{3,2,1,0:T(8,128)}) custom-call(bf16[256,128]{1,0:T(8,128)(2,1)S(1)} %bitcast.8, bf16[16,384,384]{2,1,0:T(8,128)(2,1)S(1)} %bitcast.7, bf16[384,32]{1,0:T(8,128)(2,1)S(1)} %copy-done.4, bf16[32,384]{1,0:T(8,128)(2,1)S(1)} %copy-done.5, bf16[2,384,128]{2,1,0:T(8,128)(2,1)S(1)} %copy-done.2, ...), custom_call_target="tpu_custom_call" | custom-call | tf_op jit(solution)/shard_map/lines/pallas_call | solution.py:656
  37.5 10.9 %all_to_all.11 = bf16[32,8,128]{2,1,0:T(8,128)(2,1)S(1)} all-to-all(bf16[32,8,128]{2,1,0:T(8,128)(2,1)S(1)} %bitcast.11), channel_id=1, replica_groups=mesh['fine'=32,'coarse'=4] {'fine'}, dimensions={0} | all-to-all | bytes 131072 | tf_op jit(solution)/shard_map/all_to_all | solution.py:674
  48.4 0.0 copy-done.3
  48.4 1.2 %correct.1 = f32[12,8,8,256]{3,2,1,0:T(8,128)} custom-call(f32[12,8,8,256]{3,2,1,0:T(8,128)S(1)} %get-tuple-element.23.loads_ref.low_ref.high_ref, bf16[256,128]{1,0:T(8,128)(2,1)S(1)} %bitcast.9, bf16[384,128]{1,0:T(8,128)(2,1)S(1)} %copy-done.3, bf16[2,256,256]{2,1,0:T(8,128)(2,1)S(1)} %copy-done), custom_call_target="tpu_custom_call" | custom-call | tf_op jit(solution)/shard_map/correct/pallas_call | solution.py:675
  (1 shorter events, 0.0 us)
Async XLA Ops:
  1.7 14.9 %copy-start = (bf16[2,256,256]{2,1,0:T(8,128)(2,1)S(1)}, bf16[2,256,256]{2,1,0:T(8,128)(2,1)}, u32[]{:S(2)}) copy-start(bf16[2,256,256]{2,1,0:T(8,128)(2,1)} %constant.16.clone.lift_ref) | copy-start | bytes 786436
  1.7 7.1 %collective-permute-start = (bf16[21,8,256]{2,1,0:T(8,128)(2,1)S(1)}, bf16[21,8,256]{2,1,0:T(8,128)(2,1)S(1)}, u32[]{:S(2)}, u32[]{:S(2)}) collective-permute-start(bf16[21,8,256]{2,1,0:T(8,128)(2,1)S(1)} %get-tuple-element.30), channel_id=1, source_target_pairs={{0,4},{4,0},{8,12},{12,8},{16,20},{20,16},{24,28},{28,24},{32,36},... | collective-permute-start | bytes 258056 | tf_op jit(solution)/shard_map/ppermute | solution.py:565
  2.5 6.4 %collective-permute-start.1 = (bf16[21,8,256]{2,1,0:T(8,128)(2,1)S(1)}, bf16[21,8,256]{2,1,0:T(8,128)(2,1)S(1)}, u32[]{:S(2)}, u32[]{:S(2)}) collective-permute-start(bf16[21,8,256]{2,1,0:T(8,128)(2,1)S(1)} %get-tuple-element.31), channel_id=1, source_target_pairs={{0,0},{4,8},{8,4},{12,16},{16,12},{20,24},{24,20},{28,32},{32,28},... | collective-permute-start | bytes 258056 | tf_op jit(solution)/shard_map/ppermute | solution.py:566
  5.5 28.9 %slice-start = ((s8[4718592]{0:T(1024)(128)(4,1)}), s8[4194304]{0:T(1024)(128)(4,1)S(1)}, s32[]{:S(2)}) async-start(s8[4718592]{0:T(1024)(128)(4,1)} %bitcast.5), calls=%async_computation.2 | async-start | bytes 8388608
  8.8 25.6 %copy-start.1 = (bf16[4,256,128]{2,1,0:T(8,128)(2,1)S(1)}, bf16[4,256,128]{2,1,0:T(8,128)(2,1)}, u32[]{:S(2)}) copy-start(bf16[4,256,128]{2,1,0:T(8,128)(2,1)} %constant.15.clone.fold_ref) | copy-start | bytes 786436
  8.8 25.6 %copy-start.2 = (bf16[2,384,128]{2,1,0:T(8,128)(2,1)S(1)}, bf16[2,384,128]{2,1,0:T(8,128)(2,1)}, u32[]{:S(2)}) copy-start(bf16[2,384,128]{2,1,0:T(8,128)(2,1)} %constant.14.clone.keep_ref) | copy-start | bytes 589828
  8.8 25.6 %copy-start.4 = (bf16[384,32]{1,0:T(8,128)(2,1)S(1)}, bf16[384,32]{1,0:T(8,128)(2,1)}, u32[]{:S(2)}) copy-start(bf16[384,32]{1,0:T(8,128)(2,1)} %constant.12.clone.spread_ref) | copy-start | bytes 73732
  8.8 25.5 %copy-start.5 = (bf16[32,384]{1,0:T(8,128)(2,1)S(1)}, bf16[32,384]{1,0:T(8,128)(2,1)}, u32[]{:S(2)}) copy-start(bf16[32,384]{1,0:T(8,128)(2,1)} %constant.13.clone.gather_ref) | copy-start | bytes 73732
  8.9 7.6 %collective-permute-start.2 = (bf16[26,8,256]{2,1,0:T(8,128)(2,1)S(1)}, bf16[26,8,256]{2,1,0:T(8,128)(2,1)S(1)}, u32[]{:S(2)}, u32[]{:S(2)}) collective-permute-start(bf16[26,8,256]{2,1,0:T(8,128)(2,1)S(1)} %get-tuple-element.32), channel_id=1, source_target_pairs={{0,1},{1,0},{2,3},{3,2},{4,5},{5,4},{6,7},{7,6},{8,9},{9,8},{10,11... | collective-permute-start | bytes 319496 | tf_op jit(solution)/shard_map/ppermute | solution.py:613
  9.2 25.2 %slice-start.1 = ((s8[4718592]{0:T(1024)(128)(4,1)}), s8[524288]{0:T(1024)(128)(4,1)S(1)}, s32[]{:S(2)}) async-start(s8[4718592]{0:T(1024)(128)(4,1)} %bitcast.5), calls=%async_computation.3 | async-start | bytes 1048576
  9.2 7.4 %collective-permute-start.3 = (bf16[26,8,256]{2,1,0:T(8,128)(2,1)S(1)}, bf16[26,8,256]{2,1,0:T(8,128)(2,1)S(1)}, u32[]{:S(2)}, u32[]{:S(2)}) collective-permute-start(bf16[26,8,256]{2,1,0:T(8,128)(2,1)S(1)} %get-tuple-element.33), channel_id=1, source_target_pairs={{0,0},{1,2},{2,1},{3,3},{4,4},{5,6},{6,5},{7,7},{8,8},{9,10},{10,9... | collective-permute-start | bytes 319496 | tf_op jit(solution)/shard_map/ppermute | solution.py:614
  16.6 31.8 %copy-start.3 = (bf16[384,128]{1,0:T(8,128)(2,1)S(1)}, bf16[384,128]{1,0:T(8,128)(2,1)}, u32[]{:S(2)}) copy-start(bf16[384,128]{1,0:T(8,128)(2,1)} %constant.17.clone.grown_ref) | copy-start | bytes 294916
